TPU v7x, 32 devices: a whole 2x2x4 slice. The times are simulated.
32 devices in a mesh: real: 2 (over y), tm: 4 (over z), wafer: 4 (over x, core).
Axes of the slice: x: 2, y: 2, z: 4, core: 2. Of those that a mesh axis runs over, the one named last changes fastest.
Arguments:
- tod: float32 [8192, 4096], P(('real', 'wafer'), 'tm'), parts along dimension 0, may hold values from -6 to 6
- inv_white: float32 [4096, 8], P('wafer'), may hold values from 0.5 to 2
- modes: float32 [4096, 128], P('wafer'), may hold values from -6 to 6
- mode_counts: int32 [8], replicated, may hold values from 8 to 16, as said below
- core: float32 [8, 16, 16], replicated, may hold values from -0.0017089844 to 0.0017089844
- block_coef: float32 [8, 16], replicated, may hold values from -0.109375 to 0.109375
- block_ids: int32 [4096], P('wafer'), may hold values from 0 to 15
- band_edges: int32 [9], replicated, may hold values from 0 to 256, as said below
Outputs:
- filtered: float32 [8192, 4096], P(('real', 'wafer'), 'tm'), parts along dimension 0
There are 2 independent parts, one for each index of `real`. A program takes and returns all parts, laid end to end along the dimension named above; an argument that names none is the same for every part. Nothing has to cross between parts.
Inputs may be any that keep to these rules, and one draw needn't show every extreme that they name: band_edges[0] = 0 and band_edges[8] = 256, strictly rising; every band holds at least 16 bins. `mode_counts`: some band uses all 16 eigenvectors.
All inputs are finite; a program needn't handle non-finite values.
Results may differ from a plain program's by a relative error of at most 0.0003.
Values sent between devices are 32-bit elements; how exact they have to be, the bound alone decides.
No kernel may reach another device: no remote copies, remote signals or barrier semaphores. Data moves between devices by JAX's collectives and lax.ppermute only.
A program may use at most 128 MiB of HBM per device.

v0:
```python
import math

import jax
import jax.numpy as jnp
import numpy as np
from jax import lax
from jax.experimental import pallas as pl
from jax.experimental.pallas import tpu as pltpu
from jax.sharding import PartitionSpec as P


STEP = 256
TAIL = 256
BANDS = 8
KMAX = 16
NBLK = 16
SEGLEN = 512
BINS = 256
HALF = BINS // 2
MODES = BANDS * KMAX
COLS = BANDS * (KMAX + NBLK)
ROWS = KMAX + NBLK

F32 = jnp.float32
BF16 = jnp.bfloat16


def pieces_of(table):
    high = table.astype(BF16)
    low = (table - high.astype(np.float64)).astype(BF16)
    return jnp.asarray(high), jnp.asarray(low)


def make_tables():
    bins = np.concatenate([np.arange(0, BINS, 2), np.arange(1, BINS, 2)]).reshape(2, HALF)
    time = np.arange(STEP)
    angle = 2.0 * math.pi / SEGLEN * (time[:, None, None] * bins[None] % SEGLEN)
    forward = np.stack([np.cos(angle), -np.sin(angle)], 2).reshape(STEP, 2 * BINS)
    kept = np.arange(TAIL, SEGLEN)
    back = 2.0 * math.pi / SEGLEN * (bins[:, :, None] * kept % SEGLEN)
    factor = np.where(bins == 0, 1.0, 2.0)[:, :, None] / SEGLEN
    inverse = np.stack([factor * np.cos(back), -factor * np.sin(back)], 1).reshape(2 * BINS, STEP)
    return pieces_of(forward) + pieces_of(inverse)


def split(x):
    high = x.astype(BF16)
    return high, (x - high.astype(F32)).astype(BF16)


def three(x):
    first = x.astype(BF16).astype(F32)
    second = (x - first).astype(BF16).astype(F32)
    return jnp.concatenate([first, second, x - first - second], 0).astype(BF16)


def dot(a, b):
    return jnp.dot(a, b, preferred_element_type=F32)


def dot3(a, b):
    return dot(a[0], b[0]) + (dot(a[0], b[1]) + dot(a[1], b[0]))


def band_rows(edges, width):
    col = lax.broadcasted_iota(jnp.int32, (1, width), 1)
    odd = (col >= width // 2).astype(jnp.int32)
    bin_idx = 2 * (col & (HALF - 1)) + odd
    return [
        ((bin_idx >= edges[b]) & (bin_idx < edges[b + 1])).astype(F32) for b in range(BANDS)
    ]


def chunk_of(count, most):
    return most if count % most == 0 else count


def rows_of(ref, most=256):
    count = ref.shape[0]
    size = chunk_of(count, most)
    return [slice(start, start + size) for start in range(0, count, size)]


def started(copies):
    for copy in copies:
        copy.start()
    return copies


def waited(copies):
    for copy in copies:
        copy.wait()


def tail_kernel(tod_ref, out_ref, sem):
    first = tod_ref.shape[1] - out_ref.shape[1]
    waited(
        started(
            [
                pltpu.make_async_copy(tod_ref.at[here, first:], out_ref.at[here, :], sem.at[i])
                for i, here in enumerate(rows_of(out_ref))
            ]
        )
    )


def project_kernel(
    counts, edges, tod_ref, wt_hbm, modes_hbm, ids_hbm, fh_hbm, fl_hbm, ih_hbm, il_hbm, tail_ref,
    p_ref, v_ref, w_ref, x_ref, fh_ref, fl_ref, ih_ref, il_ref, wt_ref, modes_ref, ids_ref, sem,
):
    dets, known = x_ref.shape
    segs = p_ref.shape[0]
    chunks = rows_of(x_ref)
    chunk = dets // len(chunks)
    moves = [(wt_hbm, wt_ref), (ids_hbm, ids_ref), (modes_hbm, modes_ref)]
    moves += [(tod_ref.at[here, :known], x_ref.at[here, :]) for here in chunks]
    moves += [(fh_hbm, fh_ref), (fl_hbm, fl_ref), (ih_hbm, ih_ref), (il_hbm, il_ref)]
    copies = started(
        [pltpu.make_async_copy(a, b, sem.at[i]) for i, (a, b) in enumerate(moves)]
    )
    mask = jnp.concatenate(band_rows(edges, BINS), 0)
    mask = jnp.concatenate([mask] * 3, 0).astype(BF16)
    row = lax.broadcasted_iota(jnp.int32, (KMAX, chunk), 0)
    waited(copies[:3])
    vts = []
    for here in chunks:
        wt = wt_ref[:, here]
        modes_t = modes_ref[here, :].T
        mine = row == ids_ref[:, here]
        parts = []
        for b in range(BANDS):
            part = jnp.where(row < counts[b], modes_t[b * KMAX : (b + 1) * KMAX], 0.0)
            parts.append(part * wt[b : b + 1])
        for b in range(BANDS):
            parts.append(jnp.where(mine, wt[b : b + 1], 0.0))
        vt = jnp.concatenate(parts, 0)
        v_ref[here, :COLS], v_ref[here, COLS:] = split(vt.T)
        vts.append(vt)
        w_ref[here, :] = lax.dot_general(
            three(wt), mask, (((0,), (0,)), ((), ())), preferred_element_type=F32
        )
    waited(copies[3:])
    vt = split(jnp.concatenate(vts, 1))
    q = [dot3(vt, split(x_ref[:, at : at + STEP])) for at in range(0, known, STEP)]
    q = jnp.concatenate(q + [dot3(vt, split(tail_ref[...]))], 0)
    g = dot3(split(q), (fh_ref[...], fl_ref[...]))
    masks = band_rows(edges, 2 * BINS)
    for j in range(segs):
        for part_idx in range(2):
            total = 0.0
            for b in range(BANDS):
                at = j * COLS + part_idx * MODES + b * KMAX
                total += masks[b] * g[at : at + KMAX]
            p_ref[j, part_idx * KMAX : (part_idx + 1) * KMAX, :] = total


def filtered(pairs, w, tables):
    fh, fl, ih, il = tables
    sums = split(jnp.concatenate([early + late for early, late in pairs], 0))
    gaps = split(jnp.concatenate([early - late for early, late in pairs], 0))
    even = dot3(sums, (fh[:, :BINS], fl[:, :BINS]))
    odd = dot3(gaps, (fh[:, BINS:], fl[:, BINS:]))
    we = jnp.concatenate([jnp.concatenate([w[:, :HALF]] * 2, 1)] * len(pairs), 0)
    wo = jnp.concatenate([jnp.concatenate([w[:, HALF:]] * 2, 1)] * len(pairs), 0)
    return dot3(split(even * we), (ih[:BINS], il[:BINS])) + dot3(
        split(odd * wo), (ih[BINS:], il[BINS:])
    )


def main_kernel(x_ref, tail_ref, w_ref, fh_ref, fl_ref, ih_ref, il_ref, out_ref):
    tables = fh_ref[...], fl_ref[...], ih_ref[...], il_ref[...]
    known = x_ref.shape[1]
    for here in rows_of(x_ref, 512):
        blocks = [x_ref[here, at : at + STEP] for at in range(0, known, STEP)]
        blocks.append(tail_ref[here, :])
        y = filtered(list(zip(blocks, blocks[1:])), w_ref[here, :], tables)
        chunk = here.stop - here.start
        for seg in range(len(blocks) - 1):
            out_ref[here, seg * STEP : (seg + 1) * STEP] = y[seg * chunk : (seg + 1) * chunk]


def to_correct(edges, before, after, core, coef):
    masks = band_rows(edges, 2 * BINS)
    sums = jnp.concatenate(
        [before[:, :BINS] + after[:, :BINS], before[:, BINS:] - after[:, BINS:]], 1
    )
    core = jnp.concatenate([core[b] for b in range(BANDS)], 0)
    mixed = dot3(split(core), split(sums[:KMAX]))
    mask = jnp.concatenate(masks * 3, 0).astype(BF16)
    levels = lax.dot_general(
        three(coef), mask, (((0,), (0,)), ((), ())), preferred_element_type=F32
    )
    blocks = levels * sums[KMAX:]
    parts = [masks[b] * mixed[b * KMAX : (b + 1) * KMAX] for b in range(BANDS)]
    return jnp.concatenate(parts + [masks[b] * blocks for b in range(BANDS)], 0)


def rest_kernel(
    edges, core_hbm, coef_hbm, main_ref, p_ref, q_ref, v_ref, ih_ref, il_ref,
    out_ref, core_ref, coef_ref, buf, sem,
):
    segs = p_ref.shape[0]
    waited(
        started(
            [
                pltpu.make_async_copy(core_hbm, core_ref, sem.at[0]),
                pltpu.make_async_copy(coef_hbm, coef_ref, sem.at[1]),
            ]
        )
    )
    sums = [p_ref[j] + q_ref[j] for j in range(segs)]
    core, coef = core_ref[...], coef_ref[...]
    rows = [to_correct(edges, a, b, core, coef) for a, b in zip(sums, sums[1:])]
    z = dot3(split(jnp.concatenate(rows, 0)), (ih_ref[...], il_ref[...]))
    z = split(jnp.concatenate([z[g * COLS : (g + 1) * COLS] for g in range(segs - 1)], 1))
    copies = []
    for i, here in enumerate(rows_of(buf)):
        buf[here, :] = main_ref[here, :] - dot3((v_ref[here, :COLS], v_ref[here, COLS:]), z)
        copies += started(
            [pltpu.make_async_copy(buf.at[here, :], out_ref.at[here, STEP:], sem.at[2 + i])]
        )
    waited(copies)


def first_kernel(
    edges, core_hbm, coef_hbm, tod_ref, _, odd_ref, even_ref, w_ref, v_ref, before_ref, p_ref,
    q_ref, fh_ref, fl_ref, ih_ref, il_ref, out_ref, core_ref, coef_ref, x_ref, buf, sem,
):
    tables = fh_ref[...], fl_ref[...], ih_ref[...], il_ref[...]
    place = lax.axis_index("tm")
    follows = place > 0
    here_odd = place % 2 == 1
    chunks = rows_of(buf)

    late_copy = pltpu.make_async_copy(tod_ref.at[:, :STEP], x_ref, sem.at[2 + len(chunks)])
    late_copy.start()
    waited(
        started(
            [
                pltpu.make_async_copy(core_hbm, core_ref, sem.at[0]),
                pltpu.make_async_copy(coef_hbm, coef_ref, sem.at[1]),
            ]
        )
    )
    before = jnp.where(follows, before_ref[...], 0.0)
    rows = to_correct(edges, before, p_ref[0] + q_ref[0], core_ref[...], coef_ref[...])
    z = split(dot3(split(rows), tables[2:]))
    late_copy.wait()
    copies = []
    for i, here in enumerate(chunks):
        tail = jnp.where(here_odd, odd_ref[here, :], even_ref[here, :])
        tail = jnp.where(follows, tail, 0.0)
        y = filtered([(tail, x_ref[here, :])], w_ref[here, :], tables)
        buf[here, :] = y - dot3((v_ref[here, :COLS], v_ref[here, COLS:]), z)
        copies += started(
            [pltpu.make_async_copy(buf.at[here, :], out_ref.at[here, :STEP], sem.at[2 + i])]
        )
    waited(copies)


IN_VMEM = pl.BlockSpec(memory_space=pltpu.VMEM)
ANYWHERE = pl.BlockSpec(memory_space=pl.ANY)


def run(kernel, scalars, loose, kept, outs, scratch=(), alias=None, flops=0, nbytes=0, mib=24):
    loose = [pltpu.with_memory_space_constraint(a, pltpu.HBM) for a in loose]
    kept = [pltpu.with_memory_space_constraint(a, pltpu.VMEM) for a in kept]
    many = isinstance(outs, tuple)
    places = tuple(
        ANYWHERE if isinstance(o, jax.ShapeDtypeStruct) else IN_VMEM for o in (outs if many else (outs,))
    )
    return pl.pallas_call(
        kernel,
        out_shape=outs,
        grid_spec=pltpu.PrefetchScalarGridSpec(
            num_scalar_prefetch=len(scalars),
            grid=(),
            in_specs=[ANYWHERE] * len(loose) + [IN_VMEM] * len(kept),
            out_specs=places if many else places[0],
            scratch_shapes=list(scratch),
        ),
        input_output_aliases=alias or {},
        cost_estimate=pl.CostEstimate(flops=flops, bytes_accessed=nbytes, transcendentals=0),
        compiler_params=pltpu.CompilerParams(vmem_limit_bytes=mib << 20),
    )(*scalars, *loose, *kept)


def exchanged(block, axis, distance):
    devices = range(lax.axis_size(axis))
    return lax.ppermute(block, axis, [(i, i ^ distance) for i in devices])


def pair_swap(block, parity):
    n, m = lax.axis_size("tm"), lax.axis_size("wafer")
    route = []
    for t in range(n):
        mate = t + 1 if t % 2 == parity else t - 1
        for w in range(m):
            near = w ^ 1 if w ^ 1 < m else w
            to = (mate, w) if 0 <= mate < n else (t, near)
            route.append((t * m + w, to[0] * m + to[1]))
    return lax.ppermute(block, ("tm", "wafer"), route)


def local(tod, inv_white, modes, mode_counts, core, block_coef, block_ids, band_edges):
    dets, samples = tod.shape
    segs = samples // STEP
    known = samples - TAIL
    tables = make_tables()
    along = lax.axis_size("tm")
    count = dets // chunk_of(dets, 256)
    whole = jax.ShapeDtypeStruct((dets, samples), F32)
    small = [pltpu.VMEM(core.shape, F32), pltpu.VMEM((BANDS, NBLK), F32)]

    tail = run(
        tail_kernel,
        (),
        (tod,),
        (),
        pltpu.VMEM((dets, TAIL), F32),
        scratch=[pltpu.SemaphoreType.DMA((count,))],
        nbytes=8 * dets * TAIL,
    )
    odd = pair_swap(tail, 0)
    even = pair_swap(tail, 1)

    sums, v, w, x, *tables = run(
        project_kernel,
        (mode_counts, band_edges),
        (tod, inv_white.T, modes, block_ids.reshape(1, dets), *tables),
        (tail,),
        (
            pltpu.VMEM((segs, ROWS, 2 * BINS), F32),
            pltpu.VMEM((dets, 2 * COLS), BF16),
            pltpu.VMEM((dets, BINS), F32),
            pltpu.VMEM((dets, known), F32),
            *[pltpu.VMEM(t.shape, BF16) for t in tables],
        ),
        scratch=[
            pltpu.VMEM((BANDS, dets), F32),
            pltpu.VMEM((dets, MODES), F32),
            pltpu.VMEM((1, dets), jnp.int32),
            pltpu.SemaphoreType.DMA((count + 7,)),
        ],
        flops=6 * dets * COLS * samples,
        nbytes=4 * dets * samples,
    )
    main = run(
        main_kernel,
        (),
        (),
        (x, tail, w, *tables),
        pltpu.VMEM((dets, known), F32),
        flops=24 * dets * STEP * known,
        nbytes=7 * dets * samples,
    )

    own, other, distance = sums, jnp.zeros_like(sums), 1
    while distance < lax.axis_size("wafer"):
        own = own + other if distance > 1 else own
        other = exchanged(own, "wafer", distance)
        distance *= 2
    last = own[segs - 1] + other[segs - 1]
    before = lax.ppermute(last, "tm", [(i, (i + 1) % along) for i in range(along)])

    rest = run(
        rest_kernel,
        (band_edges,),
        (core, block_coef),
        (main, own, other, v, *tables[2:]),
        whole,
        scratch=[
            *small,
            pltpu.VMEM((dets, known), F32),
            pltpu.SemaphoreType.DMA((count + 2,)),
        ],
        flops=6 * dets * COLS * known,
        nbytes=4 * dets * samples,
    )
    return run(
        first_kernel,
        (band_edges,),
        (core, block_coef, tod, rest),
        (odd, even, w, v, before, own, other, *tables),
        whole,
        scratch=[
            *small,
            pltpu.VMEM((dets, STEP), F32),
            pltpu.VMEM((dets, STEP), F32),
            pltpu.SemaphoreType.DMA((count + 3,)),
        ],
        alias={4: 0},
        flops=30 * dets * STEP * STEP,
        nbytes=4 * dets * STEP,
    )


def solution(mesh):
    return jax.shard_map(
        local,
        mesh=mesh,
        in_specs=(
            P(("real", "wafer"), "tm"),
            P("wafer", None),
            P("wafer", None),
            P(),
            P(),
            P(),
            P("wafer"),
            P(),
        ),
        out_specs=P(("real", "wafer"), "tm"),
        check_vma=False,
    )
```

profile of v0, /device:TPU:0, one launch (start us, length us, event | category | flops | bytes accessed | tf_op | source)
XLA Modules:
  0.0 43.8 jit_solution(13041738685271702858)
XLA Ops:
  0.0 0.0 copy-start
  0.0 0.0 copy-start.1
  0.0 1.3 %shard_map.118.tail_ref = f32[1024,256]{1,0:T(8,128)S(1)} custom-call(f32[1024,1024]{1,0:T(8,128)} %tod_ref.5), custom_call_target="tpu_custom_call" | custom-call | bytes 2097152 | tf_op jit(solution)/shard_map/pallas_call | solution.py:272
  1.3 0.0 copy-done
  1.3 0.0 copy-done.1
  1.3 5.7 %shard_map.119 = (f32[4,32,512]{2,1,0:T(8,128)S(1)}, bf16[1024,512]{1,0:T(8,128)(2,1)S(1)}, f32[1024,256]{1,0:T(8,128)S(1)}, f32[1024,768]{1,0:T(8,128)S(1)}, bf...) custom-call(s32[8]{0:T(128)S(1)} %copy-done.1, ...), custom_call_target="tpu_custom_call" | custom-call | flops 1610612736 | bytes 4194304 | tf_op jit(solution)/shard_map/pallas_call | solution.py:272
  7.0 0.6 %collective-permute-start = (f32[4,32,512]{2,1,0:T(8,128)S(1)}, f32[4,32,512]{2,1,0:T(8,128)S(1)}, u32[]{:S(2)}, u32[]{:S(2)}) collective-permute-start(f32[4,32,512]{2,1,0:T(8,128)S(1)} %get-tuple-element.19), channel_id=1, source_target_pairs={{0,1},{1,0},{2,3},{3,2},{4,5},{5,4},{6,7},{7,6},{8,9},{9,8},{10,11... | collective-permute-start | bytes 786440 | tf_op jit(solution)/shard_map/ppermute | solution.py:290
  7.6 0.1 collective-permute-start.3
  7.7 4.1 %collective-permute-start.2 = (f32[1024,256]{1,0:T(8,128)S(1)}, f32[1024,256]{1,0:T(8,128)S(1)}, u32[]{:S(2)}, u32[]{:S(2)}) collective-permute-start(f32[1024,256]{1,0:T(8,128)S(1)} %shard_map.118.tail_ref), channel_id=1, source_target_pairs={{0,4},{1,5},{2,6},{3,7},{4,0},{5,1},{6,2},{7,3},{8,12},{9,13},{10,... | collective-permute-start | bytes 3145736 | tf_op jit(solution)/shard_map/ppermute | solution.py:302
  11.8 0.0 collective-permute-done
  11.9 1.6 %collective-permute-start.1 = (f32[4,32,512]{2,1,0:T(8,128)S(1)}, f32[4,32,512]{2,1,0:T(8,128)S(1)}, u32[]{:S(2)}, u32[]{:S(2)}) collective-permute-start(f32[4,32,512]{2,1,0:T(8,128)S(1)} %add.9.p_ref), channel_id=1, source_target_pairs={{0,2},{1,3},{2,0},{3,1},{4,6},{5,7},{6,4},{7,5},{8,10},{9,11},{10,... | collective-permute-start | bytes 786440 | tf_op jit(solution)/shard_map/ppermute | solution.py:290
  13.4 6.1 %shard_map.120.main_ref = f32[1024,768]{1,0:T(8,128)S(1)} custom-call(f32[1024,768]{1,0:T(8,128)S(1)} %get-tuple-element.13.x_ref, f32[1024,256]{1,0:T(8,128)S(1)} %shard_map.118.tail_ref, f32[1024,256]{1,0:T(8,128)S(1)} %get-tuple-element.14.w_ref, bf16[256,512]{1,0:T(8,128)(2,1)S(1)} %get-tuple-element.15.fh_ref, ...), custom_call_target="tpu_custom_call" | custom-call | flops 4831838208 | bytes 7340032 | tf_op jit(solution)/shard_map/pallas_call | solution.py:272
  19.5 0.5 %collective-permute-done.1.q_ref = f32[4,32,512]{2,1,0:T(8,128)S(1)} collective-permute-done((f32[4,32,512]{2,1,0:T(8,128)S(1)}, f32[4,32,512]{2,1,0:T(8,128)S(1)}, u32[]{:S(2)}, u32[]{:S(2)}) %collective-permute-start.1) | collective-permute-done | bytes 262176 | tf_op jit(solution)/shard_map/ppermute | solution.py:290
  20.0 0.5 %collective-permute-start.4 = (f32[32,512]{1,0:T(8,128)S(1)}, f32[32,512]{1,0:T(8,128)S(1)}, u32[]{:S(2)}, u32[]{:S(2)}) collective-permute-start(f32[32,512]{1,0:T(8,128)S(1)} %fusion), channel_id=1, source_target_pairs={{0,4},{4,8},{8,12},{12,0},{1,5},{5,9},{9,13},{13,1},{2,6},{6,10},{... | collective-permute-start | bytes 196616 | tf_op jit(solution)/shard_map/ppermute | solution.py:364
  20.5 5.8 %shard_map.121._ = f32[1024,1024]{1,0:T(8,128)} custom-call(s32[9]{0:T(128)S(1)} %copy-done, f32[8,16,16]{2,1,0:T(8,128)} %core_hbm.3, f32[8,16]{1,0:T(8,128)} %coef_hbm.3, f32[1024,768]{1,0:T(8,128)S(1)} %shard_map.120.main_ref, f32[4,32,512]{2,1,0:T(8,128)S(1)} %add.9.p_ref, f32[4,32,512]{2,1,0:T(8,128)S(1)} %collective-permute-done.1.q_ref, ...), custom_call_target="tpu_custom_call" | custom-call | flops 1207959552 | bytes 4194304 | tf_op jit(solution)/shard_map/pallas_call | solution.py:272
  26.4 11.4 %collective-permute-done.4.before_ref = f32[32,512]{1,0:T(8,128)S(1)} collective-permute-done((f32[32,512]{1,0:T(8,128)S(1)}, f32[32,512]{1,0:T(8,128)S(1)}, u32[]{:S(2)}, u32[]{:S(2)}) %collective-permute-start.4) | collective-permute-done | bytes 65568 | tf_op jit(solution)/shard_map/ppermute | solution.py:364
  37.7 0.0 collective-permute-done.3.even_ref
  37.8 0.0 collective-permute-done.2.odd_ref
  37.8 5.9 %shard_map.122 = f32[1024,1024]{1,0:T(8,128)} custom-call(s32[9]{0:T(128)S(1)} %copy-done, f32[8,16,16]{2,1,0:T(8,128)} %core_hbm.3, f32[8,16]{1,0:T(8,128)} %coef_hbm.3, f32[1024,1024]{1,0:T(8,128)} %tod_ref.5, f32[1024,1024]{1,0:T(8,128)} %shard_map.121._, f32[1024,256]{1,0:T(8,128)S(1)} %collective-permute-done.2.odd_ref, ...), custom_call_target="tpu_custom_call", output_to_operand_aliasing={{}: (4, {})} | custom-call | flops 2013265920 | bytes 1048576 | tf_op jit(solution)/shard_map/pallas_call | solution.py:272
  (2 shorter events, 0.1 us)
Async XLA Ops:
  0.0 1.3 %copy-start = (s32[9]{0:T(128)S(1)}, s32[9]{0:T(128)}, u32[]{:S(2)}) copy-start(s32[9]{0:T(128)} %edges.5) | copy-start | bytes 112
  0.0 1.3 %copy-start.1 = (s32[8]{0:T(128)S(1)}, s32[8]{0:T(128)}, u32[]{:S(2)}) copy-start(s32[8]{0:T(128)} %counts.1) | copy-start | bytes 100
  7.0 4.8 %collective-permute-start = (f32[4,32,512]{2,1,0:T(8,128)S(1)}, f32[4,32,512]{2,1,0:T(8,128)S(1)}, u32[]{:S(2)}, u32[]{:S(2)}) collective-permute-start(f32[4,32,512]{2,1,0:T(8,128)S(1)} %get-tuple-element.19), channel_id=1, source_target_pairs={{0,1},{1,0},{2,3},{3,2},{4,5},{5,4},{6,7},{7,6},{8,9},{9,8},{10,11... | collective-permute-start | bytes 786440 | tf_op jit(solution)/shard_map/ppermute | solution.py:290
  7.6 30.2 %collective-permute-start.3 = (f32[1024,256]{1,0:T(8,128)S(1)}, f32[1024,256]{1,0:T(8,128)S(1)}, u32[]{:S(2)}, u32[]{:S(2)}) collective-permute-start(f32[1024,256]{1,0:T(8,128)S(1)} %shard_map.118.tail_ref), channel_id=1, source_target_pairs={{0,1},{1,0},{2,3},{3,2},{4,8},{5,9},{6,10},{7,11},{8,4},{9,5},{10,... | collective-permute-start | bytes 3145736 | tf_op jit(solution)/shard_map/ppermute | solution.py:302
  7.7 30.1 %collective-permute-start.2 = (f32[1024,256]{1,0:T(8,128)S(1)}, f32[1024,256]{1,0:T(8,128)S(1)}, u32[]{:S(2)}, u32[]{:S(2)}) collective-permute-start(f32[1024,256]{1,0:T(8,128)S(1)} %shard_map.118.tail_ref), channel_id=1, source_target_pairs={{0,4},{1,5},{2,6},{3,7},{4,0},{5,1},{6,2},{7,3},{8,12},{9,13},{10,... | collective-permute-start | bytes 3145736 | tf_op jit(solution)/shard_map/ppermute | solution.py:302
  11.9 8.1 %collective-permute-start.1 = (f32[4,32,512]{2,1,0:T(8,128)S(1)}, f32[4,32,512]{2,1,0:T(8,128)S(1)}, u32[]{:S(2)}, u32[]{:S(2)}) collective-permute-start(f32[4,32,512]{2,1,0:T(8,128)S(1)} %add.9.p_ref), channel_id=1, source_target_pairs={{0,2},{1,3},{2,0},{3,1},{4,6},{5,7},{6,4},{7,5},{8,10},{9,11},{10,... | collective-permute-start | bytes 786440 | tf_op jit(solution)/shard_map/ppermute | solution.py:290
  20.0 17.7 %collective-permute-start.4 = (f32[32,512]{1,0:T(8,128)S(1)}, f32[32,512]{1,0:T(8,128)S(1)}, u32[]{:S(2)}, u32[]{:S(2)}) collective-permute-start(f32[32,512]{1,0:T(8,128)S(1)} %fusion), channel_id=1, source_target_pairs={{0,4},{4,8},{8,12},{12,0},{1,5},{5,9},{9,13},{13,1},{2,6},{6,10},{... | collective-permute-start | bytes 196616 | tf_op jit(solution)/shard_map/ppermute | solution.py:364
where the time goes:
time: 44 us; the launch traced here: 43.8 us
  Pallas kernels  24.8 us (56%)
  waiting for transfers between devices  11.9 us (27%)
  starting transfers between devices  6.85 us (16%)
    pallas_call x5, Pallas kernels, run(): pl.pallas_call(kernel, out_shape=outs, grid_spec=pltpu.PrefetchScalarGrid...  24.8 us
    ppermute x1, waiting for transfers between devices, local(): lax.ppermute(last, 'tm', [(i, (i + 1) % along) for i in range(along)])  11.4 us
    ppermute x2, starting transfers between devices, pair_swap(): return lax.ppermute(block, ('tm', 'wafer'), route)  4.21 us
    ppermute x2, starting transfers between devices, exchanged(): return lax.ppermute(block, axis, [(i, i ^ distance) for i in devices])  2.12 us
  transfers between devices with their start and end apart: 5, of which 2 were waited for; matrix products, arithmetic and copies ran while one was open for 0% of the time, Pallas kernels for 27%

commit v1 on v0

v1 whole, which is shorter than its diff:
```python
import math

import jax
import jax.numpy as jnp
import numpy as np
from jax import lax
from jax.experimental import pallas as pl
from jax.experimental.pallas import tpu as pltpu
from jax.sharding import PartitionSpec as P


STEP = 256
TAIL = 256
BANDS = 8
KMAX = 16
NBLK = 16
SEGLEN = 512
BINS = 256
HALF = BINS // 2
MODES = BANDS * KMAX
COLS = BANDS * (KMAX + NBLK)
ROWS = KMAX + NBLK

F32 = jnp.float32
BF16 = jnp.bfloat16


def pieces_of(table):
    high = table.astype(BF16)
    low = (table - high.astype(np.float64)).astype(BF16)
    return jnp.asarray(high), jnp.asarray(low)


def make_tables():
    bins = np.concatenate([np.arange(0, BINS, 2), np.arange(1, BINS, 2)]).reshape(2, HALF)
    time = np.arange(STEP)
    angle = 2.0 * math.pi / SEGLEN * (time[:, None, None] * bins[None] % SEGLEN)
    forward = np.stack([np.cos(angle), -np.sin(angle)], 2).reshape(STEP, 2 * BINS)
    kept = np.arange(TAIL, SEGLEN)
    back = 2.0 * math.pi / SEGLEN * (bins[:, :, None] * kept % SEGLEN)
    factor = np.where(bins == 0, 1.0, 2.0)[:, :, None] / SEGLEN
    inverse = np.stack([factor * np.cos(back), -factor * np.sin(back)], 1).reshape(2 * BINS, STEP)
    return pieces_of(forward) + pieces_of(inverse)


def split(x):
    high = x.astype(BF16)
    return high, (x - high.astype(F32)).astype(BF16)


def three(x):
    first = x.astype(BF16).astype(F32)
    second = (x - first).astype(BF16).astype(F32)
    return jnp.concatenate([first, second, x - first - second], 0).astype(BF16)


def dot(a, b):
    return jnp.dot(a, b, preferred_element_type=F32)


def dot3(a, b):
    return dot(a[0], b[0]) + (dot(a[0], b[1]) + dot(a[1], b[0]))


def band_rows(edges, width):
    col = lax.broadcasted_iota(jnp.int32, (1, width), 1)
    odd = (col >= width // 2).astype(jnp.int32)
    bin_idx = 2 * (col & (HALF - 1)) + odd
    rows = [
        (bin_idx >= edges[:, b : b + 1]) & (bin_idx < edges[:, b + 1 : b + 2])
        for b in range(BANDS)
    ]
    return jnp.concatenate([row.astype(F32) for row in rows], 0)


def chunk_of(count, most):
    return most if count % most == 0 else count


def rows_of(ref, most=256):
    count = ref.shape[0]
    size = chunk_of(count, most)
    return [slice(start, start + size) for start in range(0, count, size)]


def started(copies):
    for copy in copies:
        copy.start()
    return copies


def waited(copies):
    for copy in copies:
        copy.wait()


def load_kernel(tod_ref, *refs):
    count = (len(refs) - 3) // 2
    small, (soon_ref, late_ref), kept, sem = refs[:count], refs[count : count + 2], refs[count + 2 : -1], refs[-1]
    first = tod_ref.shape[1] - TAIL
    moves, done = [], 0
    for part in (soon_ref, late_ref):
        for here in rows_of(part):
            there = slice(done + here.start, done + here.stop)
            moves.append((tod_ref.at[there, first:], part.at[here, :]))
        done += part.shape[0]
    moves += list(zip(small, kept))
    waited(
        started([pltpu.make_async_copy(a, b, sem.at[i]) for i, (a, b) in enumerate(moves)])
    )


def project_kernel(
    tod_ref, wt_ref, modes_ref, ids_ref, counts_ref, edges_ref, fh_ref, fl_ref,
    p_ref, vt_ref, mask_ref,
):
    segs = p_ref.shape[0]
    counts = counts_ref[...]
    mask = band_rows(edges_ref[...], 2 * BINS)
    mask_ref[...] = mask
    vts = []
    for here in rows_of(modes_ref):
        wt = wt_ref[:, here]
        modes_t = modes_ref[here, :].T
        row = lax.broadcasted_iota(jnp.int32, (KMAX, here.stop - here.start), 0)
        mine = row == ids_ref[:, here]
        parts = []
        for b in range(BANDS):
            part = jnp.where(row < counts[:, b : b + 1], modes_t[b * KMAX : (b + 1) * KMAX], 0.0)
            parts.append(part * wt[b : b + 1])
        for b in range(BANDS):
            parts.append(jnp.where(mine, wt[b : b + 1], 0.0))
        vts.append(jnp.concatenate(parts, 0))
        vt_ref[:, here] = vts[-1]
    vt = split(jnp.concatenate(vts, 1))
    q = [dot3(vt, split(tod_ref[:, j * STEP : (j + 1) * STEP])) for j in range(segs)]
    g = dot3(split(jnp.concatenate(q, 0)), (fh_ref[...], fl_ref[...]))
    for j in range(segs):
        for part_idx in range(2):
            total = 0.0
            for b in range(BANDS):
                at = j * COLS + part_idx * MODES + b * KMAX
                total += mask[b : b + 1] * g[at : at + KMAX]
            p_ref[j, part_idx * KMAX : (part_idx + 1) * KMAX, :] = total


def prepare_kernel(vt_ref, wt_ref, mask_ref, coef_ref, v_ref, w_ref, levels_ref):
    mask = jnp.concatenate([mask_ref[...]] * 3, 0).astype(BF16)
    across = (((0,), (0,)), ((), ()))
    levels_ref[...] = lax.dot_general(
        three(coef_ref[...]), mask, across, preferred_element_type=F32
    )
    one_each = jnp.concatenate([mask[:, :HALF], mask[:, BINS : BINS + HALF]], 1)
    for here in rows_of(v_ref):
        v_ref[here, :COLS], v_ref[here, COLS:] = split(vt_ref[:, here].T)
        w_ref[here, :] = lax.dot_general(
            three(wt_ref[:, here]), one_each, across, preferred_element_type=F32
        )


def filtered(pairs, w, tables):
    fh, fl, ih, il = tables
    sums = split(jnp.concatenate([early + late for early, late in pairs], 0))
    gaps = split(jnp.concatenate([early - late for early, late in pairs], 0))
    even = dot3(sums, (fh[:, :BINS], fl[:, :BINS]))
    odd = dot3(gaps, (fh[:, BINS:], fl[:, BINS:]))
    we = jnp.concatenate([jnp.concatenate([w[:, :HALF]] * 2, 1)] * len(pairs), 0)
    wo = jnp.concatenate([jnp.concatenate([w[:, HALF:]] * 2, 1)] * len(pairs), 0)
    return dot3(split(even * we), (ih[:BINS], il[:BINS])) + dot3(
        split(odd * wo), (ih[BINS:], il[BINS:])
    )


def main_kernel(tod_ref, w_ref, fh_ref, fl_ref, ih_ref, il_ref, out_ref):
    tables = fh_ref[...], fl_ref[...], ih_ref[...], il_ref[...]
    for here in rows_of(tod_ref, 512):
        blocks = [tod_ref[here, at : at + STEP] for at in range(0, tod_ref.shape[1], STEP)]
        y = filtered(list(zip(blocks, blocks[1:])), w_ref[here, :], tables)
        chunk = here.stop - here.start
        for seg in range(len(blocks) - 1):
            out_ref[here, seg * STEP : (seg + 1) * STEP] = y[seg * chunk : (seg + 1) * chunk]


def pack_kernel(late_ref, p_ref, q_ref, out_ref):
    late = late_ref.shape[0]
    out_ref[:late, :] = late_ref[...]
    sums = p_ref[p_ref.shape[0] - 1] + q_ref[q_ref.shape[0] - 1]
    out_ref[late : late + ROWS, :] = sums[:, :BINS]
    out_ref[late + ROWS :, :] = sums[:, BINS:]


def to_correct(mask, before, after, core, levels):
    sums = jnp.concatenate(
        [before[:, :BINS] + after[:, :BINS], before[:, BINS:] - after[:, BINS:]], 1
    )
    core = jnp.concatenate([core[b] for b in range(BANDS)], 0)
    mixed = dot3(split(core), split(sums[:KMAX]))
    blocks = levels * sums[KMAX:]
    masks = [mask[b : b + 1] for b in range(BANDS)]
    parts = [masks[b] * mixed[b * KMAX : (b + 1) * KMAX] for b in range(BANDS)]
    return jnp.concatenate(parts + [masks[b] * blocks for b in range(BANDS)], 0)


def rest_kernel(
    main_ref, p_ref, q_ref, v_ref, mask_ref, levels_ref, core_ref, ih_ref, il_ref,
    out_ref, buf, sem,
):
    segs = p_ref.shape[0]
    sums = [p_ref[j] + q_ref[j] for j in range(segs)]
    mask, levels, core = mask_ref[...], levels_ref[...], core_ref[...]
    rows = [to_correct(mask, a, b, core, levels) for a, b in zip(sums, sums[1:])]
    z = dot3(split(jnp.concatenate(rows, 0)), (ih_ref[...], il_ref[...]))
    z = split(jnp.concatenate([z[g * COLS : (g + 1) * COLS] for g in range(segs - 1)], 1))
    copies = []
    for i, here in enumerate(rows_of(buf)):
        buf[here, :] = main_ref[here, :] - dot3((v_ref[here, :COLS], v_ref[here, COLS:]), z)
        copies += started(
            [pltpu.make_async_copy(buf.at[here, :], out_ref.at[here, STEP:], sem.at[i])]
        )
    waited(copies)


def came(odd_ref, even_ref, here):
    place = lax.axis_index("tm")
    sent = jnp.where(place % 2 == 1, odd_ref[here, :], even_ref[here, :])
    return jnp.where(place > 0, sent, 0.0)


def soon_kernel(odd_ref, even_ref, tod_ref, w_ref, fh_ref, fl_ref, ih_ref, il_ref, out_ref):
    tables = fh_ref[...], fl_ref[...], ih_ref[...], il_ref[...]
    for here in rows_of(out_ref, out_ref.shape[0]):
        pair = came(odd_ref, even_ref, here), tod_ref[here, :STEP]
        out_ref[here, :] = filtered([pair], w_ref[here, :], tables)


def late_kernel(
    _, soon_ref, odd_ref, even_ref, tod_ref, w_ref, p_ref, q_ref, v_ref, mask_ref, levels_ref,
    core_ref, fh_ref, fl_ref, ih_ref, il_ref, out_ref, buf, sem,
):
    tables = fh_ref[...], fl_ref[...], ih_ref[...], il_ref[...]
    soon = soon_ref.shape[0]
    late = buf.shape[0] - soon
    before = came(odd_ref, even_ref, slice(late, late + 2 * ROWS))
    before = jnp.concatenate([before[:ROWS], before[ROWS:]], 1)
    rows = to_correct(
        mask_ref[...], before, p_ref[0] + q_ref[0], core_ref[...], levels_ref[...]
    )
    z = split(dot3(split(rows), tables[2:]))
    here = slice(soon, soon + late)
    pair = came(odd_ref, even_ref, slice(0, late)), tod_ref[here, :STEP]
    last = filtered([pair], w_ref[here, :], tables)
    copies = []
    for i, here in enumerate(rows_of(soon_ref, late * 2) + [here]):
        y = last if here.start == soon else soon_ref[here, :]
        buf[here, :] = y - dot3((v_ref[here, :COLS], v_ref[here, COLS:]), z)
        copies += started(
            [pltpu.make_async_copy(buf.at[here, :], out_ref.at[here, :STEP], sem.at[i])]
        )
    waited(copies)


IN_VMEM = pl.BlockSpec(memory_space=pltpu.VMEM)
ANYWHERE = pl.BlockSpec(memory_space=pl.ANY)


def run(kernel, loose, kept, outs, scratch=(), alias=None, flops=0, nbytes=0):
    loose = [pltpu.with_memory_space_constraint(a, pltpu.HBM) for a in loose]
    kept = [pltpu.with_memory_space_constraint(a, pltpu.VMEM) for a in kept]
    many = isinstance(outs, tuple)
    places = tuple(
        ANYWHERE if isinstance(o, jax.ShapeDtypeStruct) else IN_VMEM for o in (outs if many else (outs,))
    )
    return pl.pallas_call(
        kernel,
        out_shape=outs,
        in_specs=[ANYWHERE] * len(loose) + [IN_VMEM] * len(kept),
        out_specs=places if many else places[0],
        scratch_shapes=list(scratch),
        input_output_aliases=alias or {},
        cost_estimate=pl.CostEstimate(flops=flops, bytes_accessed=nbytes, transcendentals=0),
        compiler_params=pltpu.CompilerParams(vmem_limit_bytes=24 << 20),
    )(*loose, *kept)


def exchanged(block, axis, distance):
    devices = range(lax.axis_size(axis))
    return lax.ppermute(block, axis, [(i, i ^ distance) for i in devices])


def pair_swap(block, parity):
    n, m = lax.axis_size("tm"), lax.axis_size("wafer")
    route = []
    for t in range(n):
        mate = t + 1 if t % 2 == parity else t - 1
        for w in range(m):
            near = w ^ 1 if w ^ 1 < m else w
            to = (mate, w) if 0 <= mate < n else (t, near)
            route.append((t * m + w, to[0] * m + to[1]))
    return lax.ppermute(block, ("tm", "wafer"), route)


def local(tod, inv_white, modes, mode_counts, core, block_coef, block_ids, band_edges):
    dets, samples = tod.shape
    segs = samples // STEP
    known = samples - TAIL
    fh, fl, ih, il = tables = make_tables()
    late = dets // 8
    soon = dets - late
    whole = jax.ShapeDtypeStruct((dets, samples), F32)

    small = (
        inv_white.T,
        modes,
        block_ids.reshape(1, dets),
        mode_counts.reshape(1, BANDS),
        band_edges.reshape(1, BANDS + 1),
    )
    tail, late_tail, wt, *small = run(
        load_kernel,
        (tod, *small),
        (),
        (
            pltpu.VMEM((soon, TAIL), F32),
            pltpu.VMEM((late, TAIL), F32),
            *[pltpu.VMEM(a.shape, a.dtype) for a in small],
        ),
        scratch=[pltpu.SemaphoreType.DMA((dets // late + 8,))],
        nbytes=8 * dets * TAIL,
    )
    odd_soon = pair_swap(tail, 0)
    even_soon = pair_swap(tail, 1)

    sums, vt, mask = run(
        project_kernel,
        (),
        (tod, wt, *small, fh, fl),
        (
            pltpu.VMEM((segs, ROWS, 2 * BINS), F32),
            pltpu.VMEM((COLS, dets), F32),
            pltpu.VMEM((BANDS, 2 * BINS), F32),
        ),
        flops=6 * dets * COLS * samples,
        nbytes=4 * dets * samples,
    )
    v, w, levels = run(
        prepare_kernel,
        (),
        (vt, wt, mask, block_coef),
        (
            pltpu.VMEM((dets, 2 * COLS), BF16),
            pltpu.VMEM((dets, BINS), F32),
            pltpu.VMEM((NBLK, 2 * BINS), F32),
        ),
        flops=6 * dets * COLS * BANDS,
        nbytes=8 * dets * COLS,
    )
    main = run(
        main_kernel,
        (),
        (tod, w, *tables),
        pltpu.VMEM((dets, known), F32),
        flops=24 * dets * STEP * known,
        nbytes=7 * dets * samples,
    )

    own, other, distance = sums, jnp.zeros_like(sums), 1
    while distance < lax.axis_size("wafer"):
        own = own + other if distance > 1 else own
        other = exchanged(own, "wafer", distance)
        distance *= 2

    packed = run(
        pack_kernel,
        (),
        (late_tail, own, other),
        pltpu.VMEM((late + 2 * ROWS, TAIL), F32),
        nbytes=8 * late * TAIL,
    )
    odd_late = pair_swap(packed, 0)
    even_late = pair_swap(packed, 1)

    rest = run(
        rest_kernel,
        (),
        (main, own, other, v, mask, levels, core, ih, il),
        whole,
        scratch=[pltpu.VMEM((dets, known), F32), pltpu.SemaphoreType.DMA((16,))],
        flops=6 * dets * COLS * known,
        nbytes=4 * dets * samples,
    )
    filtered_soon = run(
        soon_kernel,
        (),
        (odd_soon, even_soon, tod, w, *tables),
        pltpu.VMEM((soon, STEP), F32),
        flops=24 * soon * STEP * STEP,
        nbytes=8 * soon * STEP,
    )
    return run(
        late_kernel,
        (rest,),
        (filtered_soon, odd_late, even_late, tod, w, own, other, v, mask, levels, core, *tables),
        whole,
        scratch=[pltpu.VMEM((dets, STEP), F32), pltpu.SemaphoreType.DMA((16,))],
        alias={0: 0},
        flops=6 * dets * STEP * STEP,
        nbytes=4 * dets * STEP,
    )


def solution(mesh):
    return jax.shard_map(
        local,
        mesh=mesh,
        in_specs=(
            P(("real", "wafer"), "tm"),
            P("wafer", None),
            P("wafer", None),
            P(),
            P(),
            P(),
            P("wafer"),
            P(),
        ),
        out_specs=P(("real", "wafer"), "tm"),
        check_vma=False,
    )
```

time: 44 us -> 33.3 us (0.76)
  waiting for transfers between devices: 11.9 us -> 4.75 us
  Pallas kernels: 24.8 us -> 20.1 us
  starting transfers between devices: 6.85 us -> 8.06 us
    ppermute x1 -> x0, waiting for transfers between devices: 11.4 us -> none  [local(): lax.ppermute(last, 'tm', [(i, (i + 1) % along) for i in range(along)])]
    pallas_call x5 -> x8, Pallas kernels: 24.8 us -> 20.1 us  [run(): pl.pallas_call(kernel, out_shape=outs, in_specs=[ANYWHERE] * len(loose) +...]
    ppermute x2 -> x4, waiting for transfers between devices: 0.01 us -> 2.96 us  [pair_swap(): return lax.ppermute(block, ('tm', 'wafer'), route)]
    ppermute x2 -> x4, starting transfers between devices: 4.21 us -> 6.43 us  [pair_swap(): return lax.ppermute(block, ('tm', 'wafer'), route)]
    ppermute x2, waiting for transfers between devices: 0.46 us -> 1.8 us  [exchanged(): return lax.ppermute(block, axis, [(i, i ^ distance) for i in devices])]
    ppermute x1 -> x0, starting transfers between devices: 0.52 us -> none  [local(): lax.ppermute(last, 'tm', [(i, (i + 1) % along) for i in range(along)])]
    ppermute x2, starting transfers between devices: 2.12 us -> 1.63 us  [exchanged(): return lax.ppermute(block, axis, [(i, i ^ distance) for i in devices])]
  transfers between devices with their start and end apart: 5 -> 6, of which waited for: 2 -> 4; matrix products, arithmetic and copies ran while one was open for 0% -> 0% of each run, Pallas kernels for 27% -> 48%
where the time goes in v1:
time: 33.3 us; the launch traced here: 33.1 us
  Pallas kernels  20.1 us (60%)
  starting transfers between devices  8.06 us (24%)
  waiting for transfers between devices  4.75 us (14%)
    pallas_call x8, Pallas kernels, run(): pl.pallas_call(kernel, out_shape=outs, in_specs=[ANYWHERE] * len(loose) +...  20.1 us
    ppermute x4, starting transfers between devices, pair_swap(): return lax.ppermute(block, ('tm', 'wafer'), route)  6.43 us
    ppermute x4, waiting for transfers between devices, pair_swap(): return lax.ppermute(block, ('tm', 'wafer'), route)  2.96 us
    ppermute x2, waiting for transfers between devices, exchanged(): return lax.ppermute(block, axis, [(i, i ^ distance) for i in devices])  1.8 us
    ppermute x2, starting transfers between devices, exchanged(): return lax.ppermute(block, axis, [(i, i ^ distance) for i in devices])  1.63 us
  transfers between devices with their start and end apart: 6, of which 4 were waited for; matrix products, arithmetic and copies ran while one was open for 0% of the time, Pallas kernels for 48%

profile of v1, /device:TPU:0, one launch (start us, length us, event | category | flops | bytes accessed | tf_op | source)
XLA Modules:
  0.0 33.1 jit_solution(7827929867550259385)
XLA Ops:
  0.0 0.0 copy-start.3
  0.0 0.0 copy-start.4
  0.0 0.0 copy-start
  0.0 0.0 copy-start.6
  0.0 1.7 %shard_map.118 = (f32[896,256]{1,0:T(8,128)S(1)}, f32[128,256]{1,0:T(8,128)S(1)}, f32[8,1024]{1,0:T(8,128)S(1)}, f32[1024,128]{1,0:T(8,128)S(1)}, s32[1,1024]{1,...) custom-call(f32[1024,1024]{1,0:T(8,128)} %tod_ref.9, f32[8,1024]{1,0:T(8,128)} %bitcast.4, f32[1024,128]{1,0:T(8,128)} %refs_1_.1, ...), custom_call_target="tpu_custom_call" | custom-call | bytes 2097152 | tf_op jit(solution)/shard_map/pallas_call | solution.py:273
  1.7 0.0 copy-start.1
  1.7 0.0 copy-start.2
  1.7 0.6 %collective-permute-start.3 = (f32[896,256]{1,0:T(8,128)S(1)}, f32[896,256]{1,0:T(8,128)S(1)}, u32[]{:S(2)}, u32[]{:S(2)}) collective-permute-start(f32[896,256]{1,0:T(8,128)S(1)} %get-tuple-element.29), channel_id=1, source_target_pairs={{0,1},{1,0},{2,3},{3,2},{4,8},{5,9},{6,10},{7,11},{8,4},{9,5},{10,... | collective-permute-start | bytes 2752520 | tf_op jit(solution)/shard_map/ppermute | solution.py:299
  2.3 4.1 %collective-permute-start.2 = (f32[896,256]{1,0:T(8,128)S(1)}, f32[896,256]{1,0:T(8,128)S(1)}, u32[]{:S(2)}, u32[]{:S(2)}) collective-permute-start(f32[896,256]{1,0:T(8,128)S(1)} %get-tuple-element.29), channel_id=1, source_target_pairs={{0,4},{1,5},{2,6},{3,7},{4,0},{5,1},{6,2},{7,3},{8,12},{9,13},{10,... | collective-permute-start | bytes 2752520 | tf_op jit(solution)/shard_map/ppermute | solution.py:299
  6.4 0.0 copy-done.3
  6.4 0.0 copy-done.4
  6.4 0.0 copy-done
  6.4 2.8 %shard_map.119 = (f32[4,32,512]{2,1,0:T(8,128)S(1)}, f32[256,1024]{1,0:T(8,128)S(1)}, f32[8,512]{1,0:T(8,128)S(1)}) custom-call(f32[1024,1024]{1,0:T(8,128)S(1)} %copy-done, f32[8,1024]{1,0:T(8,128)S(1)} %get-tuple-element.18.wt_ref, f32[1024,128]{1,0:T(8,128)S(1)} %get-tuple-element.19.modes_ref, s32[1,1024]{1,0:T(1,128)S(1)} %get-tuple-element.20.ids_ref, ...), custom_call_target="tpu_custom_call" | custom-call | flops 1610612736 | bytes 4194304 | tf_op jit(solution)/shard_map/pallas_call | solution.py:273
  9.2 0.1 collective-permute-start
  9.3 0.0 copy-done.6
  9.3 0.5 %shard_map.120 = (bf16[1024,512]{1,0:T(8,128)(2,1)S(1)}, f32[1024,256]{1,0:T(8,128)S(1)}, f32[16,512]{1,0:T(8,128)S(1)}) custom-call(f32[256,1024]{1,0:T(8,128)S(1)} %get-tuple-element.23.vt_ref, f32[8,1024]{1,0:T(8,128)S(1)} %get-tuple-element.18.wt_ref, f32[8,512]{1,0:T(8,128)S(1)} %get-tuple-element.24.mask_ref, f32[8,16]{1,0:T(8,128)S(1)} %copy-done.6), custom_call_target="tpu_custom_call" | custom-call | flops 12582912 | bytes 2097152 | tf_op jit(solution)/shard_map/pallas_call | solution.py:273
  9.8 1.0 %collective-permute-done = f32[4,32,512]{2,1,0:T(8,128)S(1)} collective-permute-done((f32[4,32,512]{2,1,0:T(8,128)S(1)}, f32[4,32,512]{2,1,0:T(8,128)S(1)}, u32[]{:S(2)}, u32[]{:S(2)}) %collective-permute-start) | collective-permute-done | bytes 262176 | tf_op jit(solution)/shard_map/ppermute | solution.py:287
  10.9 1.6 %collective-permute-start.1 = (f32[4,32,512]{2,1,0:T(8,128)S(1)}, f32[4,32,512]{2,1,0:T(8,128)S(1)}, u32[]{:S(2)}, u32[]{:S(2)}) collective-permute-start(f32[4,32,512]{2,1,0:T(8,128)S(1)} %add.3.p_ref), channel_id=1, source_target_pairs={{0,2},{1,3},{2,0},{3,1},{4,6},{5,7},{6,4},{7,5},{8,10},{9,11},{10,... | collective-permute-start | bytes 786440 | tf_op jit(solution)/shard_map/ppermute | solution.py:287
  12.4 0.0 copy-done.1
  12.4 0.0 copy-done.2
  12.4 0.0 copy-start.5
  12.4 6.1 %shard_map.121.main_ref = f32[1024,768]{1,0:T(8,128)S(1)} custom-call(f32[1024,1024]{1,0:T(8,128)S(1)} %copy-done, f32[1024,256]{1,0:T(8,128)S(1)} %get-tuple-element.25.w_ref, bf16[256,512]{1,0:T(8,128)(2,1)S(1)} %copy-done.4, bf16[256,512]{1,0:T(8,128)(2,1)S(1)} %copy-done.3, bf16[512,256]{1,0:T(8,128)(2,1)S(1)} %copy-done.2, bf16[512,256]{1,0:T(8,128)(2,1)S(1)} %copy-done.1), custom_call_target="tpu_custom_call" | custom-call | flops 4831838208 | bytes 7340032 | tf_op jit(solution)/shard_map/pallas_call | solution.py:273
  18.5 0.8 %collective-permute-done.1.q_ref = f32[4,32,512]{2,1,0:T(8,128)S(1)} collective-permute-done((f32[4,32,512]{2,1,0:T(8,128)S(1)}, f32[4,32,512]{2,1,0:T(8,128)S(1)}, u32[]{:S(2)}, u32[]{:S(2)}) %collective-permute-start.1) | collective-permute-done | bytes 262176 | tf_op jit(solution)/shard_map/ppermute | solution.py:287
  19.3 0.1 collective-permute-start.5
  19.4 1.7 %collective-permute-start.4 = (f32[192,256]{1,0:T(8,128)S(1)}, f32[192,256]{1,0:T(8,128)S(1)}, u32[]{:S(2)}, u32[]{:S(2)}) collective-permute-start(f32[192,256]{1,0:T(8,128)S(1)} %shard_map.124), channel_id=1, source_target_pairs={{0,4},{1,5},{2,6},{3,7},{4,0},{5,1},{6,2},{7,3},{8,12},{9,13},{10,... | collective-permute-start | bytes 589832 | tf_op jit(solution)/shard_map/ppermute | solution.py:299
  21.0 0.0 copy-done.5
  21.0 4.5 %shard_map.122._ = f32[1024,1024]{1,0:T(8,128)} custom-call(f32[1024,768]{1,0:T(8,128)S(1)} %shard_map.121.main_ref, f32[4,32,512]{2,1,0:T(8,128)S(1)} %add.3.p_ref, f32[4,32,512]{2,1,0:T(8,128)S(1)} %collective-permute-done.1.q_ref, bf16[1024,512]{1,0:T(8,128)(2,1)S(1)} %get-tuple-element.27.v_ref, f32[8,512]{1,0:T(8,128)S(1)} %get-tuple-element.24.mask_ref, ...), custom_call_target="tpu_custom_call" | custom-call | flops 1207959552 | bytes 4194304 | tf_op jit(solution)/shard_map/pallas_call | solution.py:273
  25.5 0.0 collective-permute-done.3.even_ref
  25.5 2.1 %collective-permute-done.2.odd_ref = f32[896,256]{1,0:T(8,128)S(1)} collective-permute-done((f32[896,256]{1,0:T(8,128)S(1)}, f32[896,256]{1,0:T(8,128)S(1)}, u32[]{:S(2)}, u32[]{:S(2)}) %collective-permute-start.2) | collective-permute-done | bytes 917536 | tf_op jit(solution)/shard_map/ppermute | solution.py:299
  27.6 2.2 %shard_map.123.soon_ref = f32[896,256]{1,0:T(8,128)S(1)} custom-call(f32[896,256]{1,0:T(8,128)S(1)} %collective-permute-done.2.odd_ref, f32[896,256]{1,0:T(8,128)S(1)} %collective-permute-done.3.even_ref, f32[1024,1024]{1,0:T(8,128)S(1)} %copy-done, f32[1024,256]{1,0:T(8,128)S(1)} %get-tuple-element.25.w_ref, bf16[256,512]{1,0:T(8,128)(2,1)S(1)} %copy-done.4, ...), custom_call_target="tpu_custom_call" | custom-call | flops 1409286144 | bytes 1835008 | tf_op jit(solution)/shard_map/pallas_call | solution.py:273
  29.8 0.0 collective-permute-done.5.even_ref
  29.8 0.9 %collective-permute-done.4.odd_ref = f32[192,256]{1,0:T(8,128)S(1)} collective-permute-done((f32[192,256]{1,0:T(8,128)S(1)}, f32[192,256]{1,0:T(8,128)S(1)}, u32[]{:S(2)}, u32[]{:S(2)}) %collective-permute-start.4) | collective-permute-done | bytes 196640 | tf_op jit(solution)/shard_map/ppermute | solution.py:299
  30.7 2.4 %shard_map.125 = f32[1024,1024]{1,0:T(8,128)} custom-call(f32[1024,1024]{1,0:T(8,128)} %shard_map.122._, f32[896,256]{1,0:T(8,128)S(1)} %shard_map.123.soon_ref, f32[192,256]{1,0:T(8,128)S(1)} %collective-permute-done.4.odd_ref, f32[192,256]{1,0:T(8,128)S(1)} %collective-permute-done.5.even_ref, ...), custom_call_target="tpu_custom_call", output_to_operand_aliasing={{}: (0, {})} | custom-call | flops 402653184 | bytes 1048576 | tf_op jit(solution)/shard_map/pallas_call | solution.py:273
  (2 shorter events, 0.1 us)
Async XLA Ops:
  0.0 6.4 %copy-start.3 = (bf16[256,512]{1,0:T(8,128)(2,1)S(1)}, bf16[256,512]{1,0:T(8,128)(2,1)}, u32[]{:S(2)}) copy-start(bf16[256,512]{1,0:T(8,128)(2,1)} %constant.9.clone.fl_ref) | copy-start | bytes 786436
  0.0 6.4 %copy-start.4 = (bf16[256,512]{1,0:T(8,128)(2,1)S(1)}, bf16[256,512]{1,0:T(8,128)(2,1)}, u32[]{:S(2)}) copy-start(bf16[256,512]{1,0:T(8,128)(2,1)} %constant.8.clone.fh_ref) | copy-start | bytes 786436
  0.0 6.4 %copy-start = (f32[1024,1024]{1,0:T(8,128)S(1)}, f32[1024,1024]{1,0:T(8,128)}, u32[]{:S(2)}) copy-start(f32[1024,1024]{1,0:T(8,128)} %tod_ref.9) | copy-start | bytes 12582916
  0.0 9.3 %copy-start.6 = (f32[8,16]{1,0:T(8,128)S(1)}, f32[8,16]{1,0:T(8,128)}, u32[]{:S(2)}) copy-start(f32[8,16]{1,0:T(8,128)} %coef_ref.1) | copy-start | bytes 1540
  1.7 10.7 %copy-start.1 = (bf16[512,256]{1,0:T(8,128)(2,1)S(1)}, bf16[512,256]{1,0:T(8,128)(2,1)}, u32[]{:S(2)}) copy-start(bf16[512,256]{1,0:T(8,128)(2,1)} %constant.11.clone.il_ref) | copy-start | bytes 786436
  1.7 10.7 %copy-start.2 = (bf16[512,256]{1,0:T(8,128)(2,1)S(1)}, bf16[512,256]{1,0:T(8,128)(2,1)}, u32[]{:S(2)}) copy-start(bf16[512,256]{1,0:T(8,128)(2,1)} %constant.10.clone.ih_ref) | copy-start | bytes 786436
  1.7 23.8 %collective-permute-start.3 = (f32[896,256]{1,0:T(8,128)S(1)}, f32[896,256]{1,0:T(8,128)S(1)}, u32[]{:S(2)}, u32[]{:S(2)}) collective-permute-start(f32[896,256]{1,0:T(8,128)S(1)} %get-tuple-element.29), channel_id=1, source_target_pairs={{0,1},{1,0},{2,3},{3,2},{4,8},{5,9},{6,10},{7,11},{8,4},{9,5},{10,... | collective-permute-start | bytes 2752520 | tf_op jit(solution)/shard_map/ppermute | solution.py:299
  2.3 25.3 %collective-permute-start.2 = (f32[896,256]{1,0:T(8,128)S(1)}, f32[896,256]{1,0:T(8,128)S(1)}, u32[]{:S(2)}, u32[]{:S(2)}) collective-permute-start(f32[896,256]{1,0:T(8,128)S(1)} %get-tuple-element.29), channel_id=1, source_target_pairs={{0,4},{1,5},{2,6},{3,7},{4,0},{5,1},{6,2},{7,3},{8,12},{9,13},{10,... | collective-permute-start | bytes 2752520 | tf_op jit(solution)/shard_map/ppermute | solution.py:299
  9.2 1.6 %collective-permute-start = (f32[4,32,512]{2,1,0:T(8,128)S(1)}, f32[4,32,512]{2,1,0:T(8,128)S(1)}, u32[]{:S(2)}, u32[]{:S(2)}) collective-permute-start(f32[4,32,512]{2,1,0:T(8,128)S(1)} %get-tuple-element.26), channel_id=1, source_target_pairs={{0,1},{1,0},{2,3},{3,2},{4,5},{5,4},{6,7},{7,6},{8,9},{9,8},{10,11... | collective-permute-start | bytes 786440 | tf_op jit(solution)/shard_map/ppermute | solution.py:287
  10.9 8.4 %collective-permute-start.1 = (f32[4,32,512]{2,1,0:T(8,128)S(1)}, f32[4,32,512]{2,1,0:T(8,128)S(1)}, u32[]{:S(2)}, u32[]{:S(2)}) collective-permute-start(f32[4,32,512]{2,1,0:T(8,128)S(1)} %add.3.p_ref), channel_id=1, source_target_pairs={{0,2},{1,3},{2,0},{3,1},{4,6},{5,7},{6,4},{7,5},{8,10},{9,11},{10,... | collective-permute-start | bytes 786440 | tf_op jit(solution)/shard_map/ppermute | solution.py:287
  12.4 8.6 %copy-start.5 = (f32[8,16,16]{2,1,0:T(8,128)S(1)}, f32[8,16,16]{2,1,0:T(8,128)}, u32[]{:S(2)}) copy-start(f32[8,16,16]{2,1,0:T(8,128)} %core_ref.3) | copy-start | bytes 24580
  19.3 10.5 %collective-permute-start.5 = (f32[192,256]{1,0:T(8,128)S(1)}, f32[192,256]{1,0:T(8,128)S(1)}, u32[]{:S(2)}, u32[]{:S(2)}) collective-permute-start(f32[192,256]{1,0:T(8,128)S(1)} %shard_map.124), channel_id=1, source_target_pairs={{0,1},{1,0},{2,3},{3,2},{4,8},{5,9},{6,10},{7,11},{8,4},{9,5},{10,... | collective-permute-start | bytes 589832 | tf_op jit(solution)/shard_map/ppermute | solution.py:299
  19.4 11.3 %collective-permute-start.4 = (f32[192,256]{1,0:T(8,128)S(1)}, f32[192,256]{1,0:T(8,128)S(1)}, u32[]{:S(2)}, u32[]{:S(2)}) collective-permute-start(f32[192,256]{1,0:T(8,128)S(1)} %shard_map.124), channel_id=1, source_target_pairs={{0,4},{1,5},{2,6},{3,7},{4,0},{5,1},{6,2},{7,3},{8,12},{9,13},{10,... | collective-permute-start | bytes 589832 | tf_op jit(solution)/shard_map/ppermute | solution.py:299

commit v2 on v1

--- a/solution.py
+++ b/solution.py
@@ -21,6 +21,7 @@
 COLS = BANDS * (KMAX + NBLK)
 ROWS = KMAX + NBLK
 
+
 F32 = jnp.float32
 BF16 = jnp.bfloat16
 
@@ -95,19 +96,14 @@
 
 
 def load_kernel(tod_ref, *refs):
-    count = (len(refs) - 3) // 2
-    small, (soon_ref, late_ref), kept, sem = refs[:count], refs[count : count + 2], refs[count + 2 : -1], refs[-1]
+    *parts, sem = refs
     first = tod_ref.shape[1] - TAIL
-    moves, done = [], 0
-    for part in (soon_ref, late_ref):
-        for here in rows_of(part):
-            there = slice(done + here.start, done + here.stop)
-            moves.append((tod_ref.at[there, first:], part.at[here, :]))
-        done += part.shape[0]
-    moves += list(zip(small, kept))
-    waited(
-        started([pltpu.make_async_copy(a, b, sem.at[i]) for i, (a, b) in enumerate(moves)])
-    )
+    copies, done = [], 0
+    for i, part in enumerate(parts):
+        there = slice(done, done + part.shape[0])
+        copies.append(pltpu.make_async_copy(tod_ref.at[there, first:], part, sem.at[i]))
+        done = there.stop
+    waited(started(copies))
 
 
 def project_kernel(
@@ -181,12 +177,12 @@
             out_ref[here, seg * STEP : (seg + 1) * STEP] = y[seg * chunk : (seg + 1) * chunk]
 
 
-def pack_kernel(late_ref, p_ref, q_ref, out_ref):
-    late = late_ref.shape[0]
-    out_ref[:late, :] = late_ref[...]
+def pack_kernel(tail_ref, p_ref, q_ref, out_ref):
+    count = tail_ref.shape[0]
+    out_ref[:count, :] = tail_ref[...]
     sums = p_ref[p_ref.shape[0] - 1] + q_ref[q_ref.shape[0] - 1]
-    out_ref[late : late + ROWS, :] = sums[:, :BINS]
-    out_ref[late + ROWS :, :] = sums[:, BINS:]
+    out_ref[count : count + ROWS, :] = sums[:, :BINS]
+    out_ref[count + ROWS :, :] = sums[:, BINS:]
 
 
 def to_correct(mask, before, after, core, levels):
@@ -202,8 +198,7 @@
 
 
 def rest_kernel(
-    main_ref, p_ref, q_ref, v_ref, mask_ref, levels_ref, core_ref, ih_ref, il_ref,
-    out_ref, buf, sem,
+    main_ref, p_ref, q_ref, v_ref, mask_ref, levels_ref, core_ref, ih_ref, il_ref, out_ref
 ):
     segs = p_ref.shape[0]
     sums = [p_ref[j] + q_ref[j] for j in range(segs)]
@@ -211,51 +206,65 @@
     rows = [to_correct(mask, a, b, core, levels) for a, b in zip(sums, sums[1:])]
     z = dot3(split(jnp.concatenate(rows, 0)), (ih_ref[...], il_ref[...]))
     z = split(jnp.concatenate([z[g * COLS : (g + 1) * COLS] for g in range(segs - 1)], 1))
-    copies = []
-    for i, here in enumerate(rows_of(buf)):
-        buf[here, :] = main_ref[here, :] - dot3((v_ref[here, :COLS], v_ref[here, COLS:]), z)
-        copies += started(
-            [pltpu.make_async_copy(buf.at[here, :], out_ref.at[here, STEP:], sem.at[i])]
-        )
-    waited(copies)
-
-
-def came(odd_ref, even_ref, here):
+    out_ref[...] = main_ref[...] - dot3((v_ref[:, :COLS], v_ref[:, COLS:]), z)
+
+
+def came(odd, even):
     place = lax.axis_index("tm")
-    sent = jnp.where(place % 2 == 1, odd_ref[here, :], even_ref[here, :])
-    return jnp.where(place > 0, sent, 0.0)
-
-
-def soon_kernel(odd_ref, even_ref, tod_ref, w_ref, fh_ref, fl_ref, ih_ref, il_ref, out_ref):
+    return jnp.where(place > 0, jnp.where(place % 2 == 1, odd, even), 0.0)
+
+
+def soon_kernel(
+    rest_ref, odd_ref, even_ref, tod_ref, w_ref, fh_ref, fl_ref, ih_ref, il_ref,
+    whole_ref, out_ref, sem,
+):
+    upper = slice(0, rest_ref.shape[0] // 2)
+    copy = pltpu.make_async_copy(rest_ref.at[upper, :], whole_ref.at[upper, STEP:], sem)
+    copy.start()
     tables = fh_ref[...], fl_ref[...], ih_ref[...], il_ref[...]
-    for here in rows_of(out_ref, out_ref.shape[0]):
-        pair = came(odd_ref, even_ref, here), tod_ref[here, :STEP]
-        out_ref[here, :] = filtered([pair], w_ref[here, :], tables)
-
-
-def late_kernel(
-    _, soon_ref, odd_ref, even_ref, tod_ref, w_ref, p_ref, q_ref, v_ref, mask_ref, levels_ref,
-    core_ref, fh_ref, fl_ref, ih_ref, il_ref, out_ref, buf, sem,
+    soon = out_ref.shape[0]
+    pair = came(odd_ref[...], even_ref[...]), tod_ref[:soon, :STEP]
+    out_ref[...] = filtered([pair], w_ref[:soon, :], tables)
+    copy.wait()
+
+
+def middle_kernel(
+    _, rest_ref, soon_ref, odd_ref, even_ref, tod_ref, w_ref, p_ref, q_ref, v_ref, mask_ref,
+    levels_ref, core_ref, fh_ref, fl_ref, ih_ref, il_ref, whole_ref, out_ref, off_ref, sem,
 ):
+    lower = slice(rest_ref.shape[0] // 2, rest_ref.shape[0])
+    copy = pltpu.make_async_copy(rest_ref.at[lower, :], whole_ref.at[lower, STEP:], sem)
+    copy.start()
     tables = fh_ref[...], fl_ref[...], ih_ref[...], il_ref[...]
-    soon = soon_ref.shape[0]
-    late = buf.shape[0] - soon
-    before = came(odd_ref, even_ref, slice(late, late + 2 * ROWS))
+    soon, done = soon_ref.shape[0], out_ref.shape[0]
+    sent = came(odd_ref[...], even_ref[...])
+    before = sent[done - soon :]
     before = jnp.concatenate([before[:ROWS], before[ROWS:]], 1)
     rows = to_correct(
         mask_ref[...], before, p_ref[0] + q_ref[0], core_ref[...], levels_ref[...]
     )
     z = split(dot3(split(rows), tables[2:]))
-    here = slice(soon, soon + late)
-    pair = came(odd_ref, even_ref, slice(0, late)), tod_ref[here, :STEP]
-    last = filtered([pair], w_ref[here, :], tables)
-    copies = []
-    for i, here in enumerate(rows_of(soon_ref, late * 2) + [here]):
-        y = last if here.start == soon else soon_ref[here, :]
-        buf[here, :] = y - dot3((v_ref[here, :COLS], v_ref[here, COLS:]), z)
-        copies += started(
-            [pltpu.make_async_copy(buf.at[here, :], out_ref.at[here, :STEP], sem.at[i])]
-        )
+    pair = sent[: done - soon], tod_ref[soon:done, :STEP]
+    own = filtered([pair], w_ref[soon:done, :], tables)
+    off = dot3((v_ref[:, :COLS], v_ref[:, COLS:]), z)
+    out_ref[:soon, :] = soon_ref[...] - off[:soon]
+    out_ref[soon:, :] = own - off[soon:done]
+    off_ref[...] = off[done:]
+    copy.wait()
+
+
+def late_kernel(
+    _, most_ref, off_ref, odd_ref, even_ref, tod_ref, w_ref, fh_ref, fl_ref, ih_ref, il_ref,
+    out_ref, buf, sem,
+):
+    done = most_ref.shape[0]
+    copies = [pltpu.make_async_copy(most_ref, out_ref.at[:done, :STEP], sem.at[0])]
+    copies[0].start()
+    tables = fh_ref[...], fl_ref[...], ih_ref[...], il_ref[...]
+    pair = came(odd_ref[...], even_ref[...]), tod_ref[done:, :STEP]
+    buf[...] = filtered([pair], w_ref[done:, :], tables) - off_ref[...]
+    copies.append(pltpu.make_async_copy(buf, out_ref.at[done:, :STEP], sem.at[1]))
+    copies[1].start()
     waited(copies)
 
 
@@ -304,8 +313,8 @@
     segs = samples // STEP
     known = samples - TAIL
     fh, fl, ih, il = tables = make_tables()
-    late = dets // 8
-    soon = dets - late
+    late = middle = dets // 8
+    soon = dets - late - middle
     whole = jax.ShapeDtypeStruct((dets, samples), F32)
 
     small = (
@@ -315,25 +324,22 @@
         mode_counts.reshape(1, BANDS),
         band_edges.reshape(1, BANDS + 1),
     )
-    tail, late_tail, wt, *small = run(
+    tails = run(
         load_kernel,
-        (tod, *small),
-        (),
-        (
-            pltpu.VMEM((soon, TAIL), F32),
-            pltpu.VMEM((late, TAIL), F32),
-            *[pltpu.VMEM(a.shape, a.dtype) for a in small],
-        ),
-        scratch=[pltpu.SemaphoreType.DMA((dets // late + 8,))],
+        (tod,),
+        (),
+        tuple(pltpu.VMEM((count, TAIL), F32) for count in (soon, middle, late)),
+        scratch=[pltpu.SemaphoreType.DMA((3,))],
+        flops=int(2e10),
         nbytes=8 * dets * TAIL,
     )
-    odd_soon = pair_swap(tail, 0)
-    even_soon = pair_swap(tail, 1)
+    odd_soon = pair_swap(tails[0], 0)
+    even_soon = pair_swap(tails[0], 1)
 
     sums, vt, mask = run(
         project_kernel,
         (),
-        (tod, wt, *small, fh, fl),
+        (tod, *small, fh, fl),
         (
             pltpu.VMEM((segs, ROWS, 2 * BINS), F32),
             pltpu.VMEM((COLS, dets), F32),
@@ -345,7 +351,7 @@
     v, w, levels = run(
         prepare_kernel,
         (),
-        (vt, wt, mask, block_coef),
+        (vt, small[0], mask, block_coef),
         (
             pltpu.VMEM((dets, 2 * COLS), BF16),
             pltpu.VMEM((dets, BINS), F32),
@@ -372,39 +378,51 @@
     packed = run(
         pack_kernel,
         (),
-        (late_tail, own, other),
-        pltpu.VMEM((late + 2 * ROWS, TAIL), F32),
-        nbytes=8 * late * TAIL,
-    )
-    odd_late = pair_swap(packed, 0)
-    even_late = pair_swap(packed, 1)
+        (tails[1], own, other),
+        pltpu.VMEM((middle + 2 * ROWS, TAIL), F32),
+        nbytes=8 * middle * TAIL,
+    )
+    odd_middle = pair_swap(packed, 0)
+    even_middle = pair_swap(packed, 1)
+    odd_late = pair_swap(tails[2], 0)
+    even_late = pair_swap(tails[2], 1)
 
     rest = run(
         rest_kernel,
         (),
         (main, own, other, v, mask, levels, core, ih, il),
-        whole,
-        scratch=[pltpu.VMEM((dets, known), F32), pltpu.SemaphoreType.DMA((16,))],
+        pltpu.VMEM((dets, known), F32),
         flops=6 * dets * COLS * known,
         nbytes=4 * dets * samples,
     )
-    filtered_soon = run(
+    partly, filtered_soon = run(
         soon_kernel,
         (),
-        (odd_soon, even_soon, tod, w, *tables),
-        pltpu.VMEM((soon, STEP), F32),
+        (rest, odd_soon, even_soon, tod, w, *tables),
+        (whole, pltpu.VMEM((soon, STEP), F32)),
+        scratch=[pltpu.SemaphoreType.DMA],
         flops=24 * soon * STEP * STEP,
         nbytes=8 * soon * STEP,
     )
+    partly, most, off = run(
+        middle_kernel,
+        (partly,),
+        (rest, filtered_soon, odd_middle, even_middle, tod, w, own, other, v, mask, levels, core, *tables),
+        (whole, pltpu.VMEM((soon + middle, STEP), F32), pltpu.VMEM((late, STEP), F32)),
+        scratch=[pltpu.SemaphoreType.DMA],
+        alias={0: 0},
+        flops=8 * dets * STEP * STEP,
+        nbytes=4 * dets * STEP,
+    )
     return run(
         late_kernel,
-        (rest,),
-        (filtered_soon, odd_late, even_late, tod, w, own, other, v, mask, levels, core, *tables),
+        (partly,),
+        (most, off, odd_late, even_late, tod, w, *tables),
         whole,
-        scratch=[pltpu.VMEM((dets, STEP), F32), pltpu.SemaphoreType.DMA((16,))],
+        scratch=[pltpu.VMEM((late, STEP), F32), pltpu.SemaphoreType.DMA((2,))],
         alias={0: 0},
-        flops=6 * dets * STEP * STEP,
-        nbytes=4 * dets * STEP,
+        flops=24 * late * STEP * STEP,
+        nbytes=8 * dets * STEP,
     )
 
 

time: 33.3 us -> 43.9 us (1.32)
  local copies, waits for them, and re-layouts: 0.03 us -> 7.91 us
  waiting for transfers between devices: 4.75 us -> 7.85 us
  Pallas kernels: 20.1 us -> 19.3 us
    unnamed x14 -> x28, local copies, waits for them, and re-layouts: 0.03 us -> 7.91 us
    ppermute x4 -> x6, waiting for transfers between devices: 2.96 us -> 7.33 us  [pair_swap(): return lax.ppermute(block, ('tm', 'wafer'), route)]
    ppermute x2, waiting for transfers between devices: 1.8 us -> 0.53 us  [exchanged(): return lax.ppermute(block, axis, [(i, i ^ distance) for i in devices])]
    pallas_call x8 -> x9, Pallas kernels: 20.1 us -> 19.3 us  [run(): pl.pallas_call(kernel, out_shape=outs, in_specs=[ANYWHERE] * len(loose) +...]
    ppermute x2, starting transfers between devices: 1.63 us -> 2.11 us  [exchanged(): return lax.ppermute(block, axis, [(i, i ^ distance) for i in devices])]
    ppermute x4 -> x6, starting transfers between devices: 6.43 us -> 6.19 us  [pair_swap(): return lax.ppermute(block, ('tm', 'wafer'), route)]
  transfers between devices with their start and end apart: 6 -> 8, of which waited for: 4 -> 3; matrix products, arithmetic and copies ran while one was open for 0% -> 0% of each run, Pallas kernels for 48% -> 35%
where the time goes in v2:
time: 43.9 us; the launch traced here: 43.5 us
  Pallas kernels  19.3 us (44%)
  starting transfers between devices  8.3 us (19%)
  local copies, waits for them, and re-layouts  7.91 us (18%)
  waiting for transfers between devices  7.85 us (18%)
    pallas_call x9, Pallas kernels, run(): pl.pallas_call(kernel, out_shape=outs, in_specs=[ANYWHERE] * len(loose) +...  19.3 us
    unnamed x28, local copies, waits for them, and re-layouts  7.91 us
    ppermute x6, waiting for transfers between devices, pair_swap(): return lax.ppermute(block, ('tm', 'wafer'), route)  7.33 us
    ppermute x6, starting transfers between devices, pair_swap(): return lax.ppermute(block, ('tm', 'wafer'), route)  6.19 us
    ppermute x2, starting transfers between devices, exchanged(): return lax.ppermute(block, axis, [(i, i ^ distance) for i in devices])  2.11 us
  transfers between devices with their start and end apart: 8, of which 3 were waited for; matrix products, arithmetic and copies ran while one was open for 0% of the time, Pallas kernels for 35%

profile of v2, /device:TPU:0, one launch (start us, length us, event | category | flops | bytes accessed | tf_op | source)
XLA Modules:
  0.0 43.5 jit_solution(3072491725471515735)
XLA Ops:
  0.0 0.0 copy-start
  0.0 2.2 %copy-done = f32[1024,1024]{1,0:T(8,128)S(1)} copy-done((f32[1024,1024]{1,0:T(8,128)S(1)}, f32[1024,1024]{1,0:T(8,128)}, u32[]{:S(2)}) %copy-start) | copy-done | bytes 4194328
  2.2 0.0 copy-start.4
  2.2 0.9 %copy-done.4 = bf16[256,512]{1,0:T(8,128)(2,1)S(1)} copy-done((bf16[256,512]{1,0:T(8,128)(2,1)S(1)}, bf16[256,512]{1,0:T(8,128)(2,1)}, u32[]{:S(2)}) %copy-start.4) | copy-done | bytes 262168
  3.1 0.0 copy-start.5
  3.1 0.9 %copy-done.5 = bf16[256,512]{1,0:T(8,128)(2,1)S(1)} copy-done((bf16[256,512]{1,0:T(8,128)(2,1)S(1)}, bf16[256,512]{1,0:T(8,128)(2,1)}, u32[]{:S(2)}) %copy-start.5) | copy-done | bytes 262168
  4.1 0.0 copy-start.8
  4.1 0.8 %copy-done.8 = f32[1024,8]{0,1:T(8,128)S(1)} copy-done((f32[1024,8]{0,1:T(8,128)S(1)}, f32[1024,8]{0,1:T(8,128)}, u32[]{:S(2)}) %copy-start.8) | copy-done | bytes 32792
  4.8 0.0 copy-start.10
  4.9 1.0 %copy-done.10 = f32[1024,128]{1,0:T(8,128)S(1)} copy-done((f32[1024,128]{1,0:T(8,128)S(1)}, f32[1024,128]{1,0:T(8,128)}, u32[]{:S(2)}) %copy-start.10) | copy-done | bytes 524312
  5.9 0.0 copy-start.11
  5.9 0.7 %copy-done.11 = s32[1024]{0:T(1024)S(1)} copy-done((s32[1024]{0:T(1024)S(1)}, s32[1024]{0:T(1024)}, u32[]{:S(2)}) %copy-start.11) | copy-done | bytes 4120
  6.6 0.0 copy-start.12
  6.6 0.7 %copy-done.12 = s32[8]{0:T(128)S(1)} copy-done((s32[8]{0:T(128)S(1)}, s32[8]{0:T(128)}, u32[]{:S(2)}) %copy-start.12) | copy-done | bytes 56
  7.2 0.0 copy-start.13
  7.2 0.7 %copy-done.13 = s32[9]{0:T(128)S(1)} copy-done((s32[9]{0:T(128)S(1)}, s32[9]{0:T(128)}, u32[]{:S(2)}) %copy-start.13) | copy-done | bytes 60
  7.9 2.8 %shard_map.118 = (f32[4,32,512]{2,1,0:T(8,128)S(1)}, f32[256,1024]{1,0:T(8,128)S(1)}, f32[8,512]{1,0:T(8,128)S(1)}) custom-call(f32[1024,1024]{1,0:T(8,128)S(1)} %copy-done, f32[8,1024]{1,0:T(8,128)S(1)} %bitcast.4, f32[1024,128]{1,0:T(8,128)S(1)} %copy-done.10, s32[1,1024]{1,0:T(1,128)S(1)} %bitcast.6, s32[1,8]{1,0:T(1,128)S(1)} %bitcast.7, ...), custom_call_target="tpu_custom_call" | custom-call | flops 1610612736 | bytes 4194304 | tf_op jit(solution)/shard_map/pallas_call | solution.py:282
  10.7 0.0 copy-start.9
  10.7 0.0 copy-start.1
  10.7 0.0 copy-start.2
  10.7 0.0 copy-start.3
  10.7 0.6 %collective-permute-start = (f32[4,32,512]{2,1,0:T(8,128)S(1)}, f32[4,32,512]{2,1,0:T(8,128)S(1)}, u32[]{:S(2)}, u32[]{:S(2)}) collective-permute-start(f32[4,32,512]{2,1,0:T(8,128)S(1)} %get-tuple-element.22), channel_id=1, source_target_pairs={{0,1},{1,0},{2,3},{3,2},{4,5},{5,4},{6,7},{7,6},{8,9},{9,8},{10,11... | collective-permute-start | bytes 786440 | tf_op jit(solution)/shard_map/ppermute | solution.py:296
  11.3 1.5 %shard_map.122 = (f32[768,256]{1,0:T(8,128)S(1)}, f32[128,256]{1,0:T(8,128)S(1)}, f32[128,256]{1,0:T(8,128)S(1)}) custom-call(f32[1024,1024]{1,0:T(8,128)} %tod_ref.11), custom_call_target="tpu_custom_call" | custom-call | flops 20000000000 | bytes 2097152 | tf_op jit(solution)/shard_map/pallas_call | solution.py:282
  12.8 2.5 %collective-permute-start.2 = (f32[768,256]{1,0:T(8,128)S(1)}, f32[768,256]{1,0:T(8,128)S(1)}, u32[]{:S(2)}, u32[]{:S(2)}) collective-permute-start(f32[768,256]{1,0:T(8,128)S(1)} %get-tuple-element.25), channel_id=1, source_target_pairs={{0,4},{1,5},{2,6},{3,7},{4,0},{5,1},{6,2},{7,3},{8,12},{9,13},{10,... | collective-permute-start | bytes 2359304 | tf_op jit(solution)/shard_map/ppermute | solution.py:308
  15.3 0.4 %collective-permute-start.3 = (f32[768,256]{1,0:T(8,128)S(1)}, f32[768,256]{1,0:T(8,128)S(1)}, u32[]{:S(2)}, u32[]{:S(2)}) collective-permute-start(f32[768,256]{1,0:T(8,128)S(1)} %get-tuple-element.25), channel_id=1, source_target_pairs={{0,1},{1,0},{2,3},{3,2},{4,8},{5,9},{6,10},{7,11},{8,4},{9,5},{10,... | collective-permute-start | bytes 2359304 | tf_op jit(solution)/shard_map/ppermute | solution.py:308
  15.7 2.7 %collective-permute-start.6 = (f32[128,256]{1,0:T(8,128)S(1)}, f32[128,256]{1,0:T(8,128)S(1)}, u32[]{:S(2)}, u32[]{:S(2)}) collective-permute-start(f32[128,256]{1,0:T(8,128)S(1)} %get-tuple-element.32), channel_id=1, source_target_pairs={{0,4},{1,5},{2,6},{3,7},{4,0},{5,1},{6,2},{7,3},{8,12},{9,13},{10,... | collective-permute-start | bytes 393224 | tf_op jit(solution)/shard_map/ppermute | solution.py:308
  18.4 0.0 copy-done.9
  18.4 0.5 %shard_map.119 = (bf16[1024,512]{1,0:T(8,128)(2,1)S(1)}, f32[1024,256]{1,0:T(8,128)S(1)}, f32[16,512]{1,0:T(8,128)S(1)}) custom-call(f32[256,1024]{1,0:T(8,128)S(1)} %get-tuple-element.19.vt_ref, f32[8,1024]{1,0:T(8,128)S(1)} %bitcast.5, f32[8,512]{1,0:T(8,128)S(1)} %get-tuple-element.20.mask_ref, f32[8,16]{1,0:T(8,128)S(1)} %copy-done.9), custom_call_target="tpu_custom_call" | custom-call | flops 12582912 | bytes 2097152 | tf_op jit(solution)/shard_map/pallas_call | solution.py:282
  18.9 0.0 collective-permute-done
  19.0 1.6 %collective-permute-start.1 = (f32[4,32,512]{2,1,0:T(8,128)S(1)}, f32[4,32,512]{2,1,0:T(8,128)S(1)}, u32[]{:S(2)}, u32[]{:S(2)}) collective-permute-start(f32[4,32,512]{2,1,0:T(8,128)S(1)} %add.3.p_ref), channel_id=1, source_target_pairs={{0,2},{1,3},{2,0},{3,1},{4,6},{5,7},{6,4},{7,5},{8,10},{9,11},{10,... | collective-permute-start | bytes 786440 | tf_op jit(solution)/shard_map/ppermute | solution.py:296
  20.5 0.0 copy-done.1
  20.5 0.0 copy-done.2
  20.5 0.0 copy-done.3
  20.5 0.0 copy-start.7
  20.5 6.1 %shard_map.120.main_ref = f32[1024,768]{1,0:T(8,128)S(1)} custom-call(f32[1024,1024]{1,0:T(8,128)S(1)} %copy-done.1, f32[1024,256]{1,0:T(8,128)S(1)} %get-tuple-element.21.w_ref, bf16[256,512]{1,0:T(8,128)(2,1)S(1)} %copy-done.4, bf16[256,512]{1,0:T(8,128)(2,1)S(1)} %copy-done.5, bf16[512,256]{1,0:T(8,128)(2,1)S(1)} %copy-done.2, bf16[512,256]{1,0:T(8,128)(2,1)S(1)} %copy-done.3), custom_call_target="tpu_custom_call" | custom-call | flops 4831838208 | bytes 7340032 | tf_op jit(solution)/shard_map/pallas_call | solution.py:282
  26.6 0.5 %collective-permute-done.1.q_ref = f32[4,32,512]{2,1,0:T(8,128)S(1)} collective-permute-done((f32[4,32,512]{2,1,0:T(8,128)S(1)}, f32[4,32,512]{2,1,0:T(8,128)S(1)}, u32[]{:S(2)}, u32[]{:S(2)}) %collective-permute-start.1) | collective-permute-done | bytes 262176 | tf_op jit(solution)/shard_map/ppermute | solution.py:296
  27.1 0.3 collective-permute-start.4
  27.5 0.0 collective-permute-start.5
  27.5 0.0 copy-done.7
  27.5 0.0 copy-start.6
  27.5 3.6 %shard_map.121.rest_ref = f32[1024,768]{1,0:T(8,128)S(1)} custom-call(f32[1024,768]{1,0:T(8,128)S(1)} %shard_map.120.main_ref, f32[4,32,512]{2,1,0:T(8,128)S(1)} %add.3.p_ref, f32[4,32,512]{2,1,0:T(8,128)S(1)} %collective-permute-done.1.q_ref, bf16[1024,512]{1,0:T(8,128)(2,1)S(1)} %get-tuple-element.23.v_ref, f32[8,512]{1,0:T(8,128)S(1)} %get-tuple-element.20.mask_ref, ...), custom_call_target="tpu_custom_call" | custom-call | flops 1207959552 | bytes 4194304 | tf_op jit(solution)/shard_map/pallas_call | solution.py:282
  31.1 2.5 %collective-permute-done.2.odd_ref = f32[768,256]{1,0:T(8,128)S(1)} collective-permute-done((f32[768,256]{1,0:T(8,128)S(1)}, f32[768,256]{1,0:T(8,128)S(1)}, u32[]{:S(2)}, u32[]{:S(2)}) %collective-permute-start.2) | collective-permute-done | bytes 786464 | tf_op jit(solution)/shard_map/ppermute | solution.py:308
  33.6 0.2 collective-permute-start.7
  33.8 0.0 collective-permute-done.3.even_ref
  33.8 0.0 copy-done.6
  33.8 2.0 %shard_map.123 = (f32[1024,1024]{1,0:T(8,128)}, f32[768,256]{1,0:T(8,128)S(1)}) custom-call(f32[1024,768]{1,0:T(8,128)S(1)} %shard_map.121.rest_ref, f32[768,256]{1,0:T(8,128)S(1)} %collective-permute-done.2.odd_ref, f32[768,256]{1,0:T(8,128)S(1)} %collective-permute-done.3.even_ref, f32[1024,1024]{1,0:T(8,128)S(1)} %copy-done.1, ...), custom_call_target="tpu_custom_call" | custom-call | flops 1207959552 | bytes 1572864 | tf_op jit(solution)/shard_map/pallas_call | solution.py:282
  35.8 4.8 %collective-permute-done.4.odd_ref = f32[192,256]{1,0:T(8,128)S(1)} collective-permute-done((f32[192,256]{1,0:T(8,128)S(1)}, f32[192,256]{1,0:T(8,128)S(1)}, u32[]{:S(2)}, u32[]{:S(2)}) %collective-permute-start.4) | collective-permute-done | bytes 196640 | tf_op jit(solution)/shard_map/ppermute | solution.py:308
  40.7 0.0 collective-permute-done.5.even_ref
  40.7 1.6 %shard_map.125 = (f32[1024,1024]{1,0:T(8,128)}, f32[896,256]{1,0:T(8,128)S(1)}, f32[128,256]{1,0:T(8,128)S(1)}) custom-call(f32[1024,1024]{1,0:T(8,128)} %get-tuple-element.26._, f32[1024,768]{1,0:T(8,128)S(1)} %shard_map.121.rest_ref, f32[768,256]{1,0:T(8,128)S(1)} %get-tuple-element.27.soon_ref, ...), custom_call_target="tpu_custom_call", output_to_operand_aliasing={{0}: (0, {})} | custom-call | flops 536870912 | bytes 1048576 | tf_op jit(solution)/shard_map/pallas_call | solution.py:282
  42.3 0.0 collective-permute-done.6.odd_ref
  42.3 0.0 collective-permute-done.7.even_ref
  42.3 1.2 %shard_map.126 = f32[1024,1024]{1,0:T(8,128)} custom-call(f32[1024,1024]{1,0:T(8,128)} %get-tuple-element.29._, f32[896,256]{1,0:T(8,128)S(1)} %get-tuple-element.30.most_ref, f32[128,256]{1,0:T(8,128)S(1)} %get-tuple-element.31.off_ref, f32[128,256]{1,0:T(8,128)S(1)} %collective-permute-done.6.odd_ref, ...), custom_call_target="tpu_custom_call", output_to_operand_aliasing={{}: (0, {})} | custom-call | flops 201326592 | bytes 2097152 | tf_op jit(solution)/shard_map/pallas_call | solution.py:282
  (2 shorter events, 0.1 us)
Async XLA Ops:
  0.0 2.2 %copy-start = (f32[1024,1024]{1,0:T(8,128)S(1)}, f32[1024,1024]{1,0:T(8,128)}, u32[]{:S(2)}) copy-start(f32[1024,1024]{1,0:T(8,128)} %tod_ref.11) | copy-start | bytes 12582916
  2.2 0.9 %copy-start.4 = (bf16[256,512]{1,0:T(8,128)(2,1)S(1)}, bf16[256,512]{1,0:T(8,128)(2,1)}, u32[]{:S(2)}) copy-start(bf16[256,512]{1,0:T(8,128)(2,1)} %constant.8.clone.fh_ref) | copy-start | bytes 786436
  3.1 0.9 %copy-start.5 = (bf16[256,512]{1,0:T(8,128)(2,1)S(1)}, bf16[256,512]{1,0:T(8,128)(2,1)}, u32[]{:S(2)}) copy-start(bf16[256,512]{1,0:T(8,128)(2,1)} %constant.9.clone.fl_ref) | copy-start | bytes 786436
  4.1 0.8 %copy-start.8 = (f32[1024,8]{0,1:T(8,128)S(1)}, f32[1024,8]{0,1:T(8,128)}, u32[]{:S(2)}) copy-start(f32[1024,8]{0,1:T(8,128)} %param.13) | copy-start | bytes 98308
  4.8 1.0 %copy-start.10 = (f32[1024,128]{1,0:T(8,128)S(1)}, f32[1024,128]{1,0:T(8,128)}, u32[]{:S(2)}) copy-start(f32[1024,128]{1,0:T(8,128)} %modes_ref.1) | copy-start | bytes 1572868
  5.9 0.7 %copy-start.11 = (s32[1024]{0:T(1024)S(1)}, s32[1024]{0:T(1024)}, u32[]{:S(2)}) copy-start(s32[1024]{0:T(1024)} %param.18) | copy-start | bytes 12292
  6.6 0.7 %copy-start.12 = (s32[8]{0:T(128)S(1)}, s32[8]{0:T(128)}, u32[]{:S(2)}) copy-start(s32[8]{0:T(128)} %param.15) | copy-start | bytes 100
  7.2 0.7 %copy-start.13 = (s32[9]{0:T(128)S(1)}, s32[9]{0:T(128)}, u32[]{:S(2)}) copy-start(s32[9]{0:T(128)} %param.19) | copy-start | bytes 112
  10.7 7.8 %copy-start.9 = (f32[8,16]{1,0:T(8,128)S(1)}, f32[8,16]{1,0:T(8,128)}, u32[]{:S(2)}) copy-start(f32[8,16]{1,0:T(8,128)} %coef_ref.1) | copy-start | bytes 1540
  10.7 9.9 %copy-start.1 = (f32[1024,1024]{1,0:T(8,128)S(1)}, f32[1024,1024]{1,0:T(8,128)}, u32[]{:S(2)}) copy-start(f32[1024,1024]{1,0:T(8,128)} %tod_ref.11) | copy-start | bytes 12582916
  10.7 9.8 %copy-start.2 = (bf16[512,256]{1,0:T(8,128)(2,1)S(1)}, bf16[512,256]{1,0:T(8,128)(2,1)}, u32[]{:S(2)}) copy-start(bf16[512,256]{1,0:T(8,128)(2,1)} %constant.10.clone.ih_ref) | copy-start | bytes 786436
  10.7 9.8 %copy-start.3 = (bf16[512,256]{1,0:T(8,128)(2,1)S(1)}, bf16[512,256]{1,0:T(8,128)(2,1)}, u32[]{:S(2)}) copy-start(bf16[512,256]{1,0:T(8,128)(2,1)} %constant.11.clone.il_ref) | copy-start | bytes 786436
  10.7 8.2 %collective-permute-start = (f32[4,32,512]{2,1,0:T(8,128)S(1)}, f32[4,32,512]{2,1,0:T(8,128)S(1)}, u32[]{:S(2)}, u32[]{:S(2)}) collective-permute-start(f32[4,32,512]{2,1,0:T(8,128)S(1)} %get-tuple-element.22), channel_id=1, source_target_pairs={{0,1},{1,0},{2,3},{3,2},{4,5},{5,4},{6,7},{7,6},{8,9},{9,8},{10,11... | collective-permute-start | bytes 786440 | tf_op jit(solution)/shard_map/ppermute | solution.py:296
  12.8 20.9 %collective-permute-start.2 = (f32[768,256]{1,0:T(8,128)S(1)}, f32[768,256]{1,0:T(8,128)S(1)}, u32[]{:S(2)}, u32[]{:S(2)}) collective-permute-start(f32[768,256]{1,0:T(8,128)S(1)} %get-tuple-element.25), channel_id=1, source_target_pairs={{0,4},{1,5},{2,6},{3,7},{4,0},{5,1},{6,2},{7,3},{8,12},{9,13},{10,... | collective-permute-start | bytes 2359304 | tf_op jit(solution)/shard_map/ppermute | solution.py:308
  15.3 18.5 %collective-permute-start.3 = (f32[768,256]{1,0:T(8,128)S(1)}, f32[768,256]{1,0:T(8,128)S(1)}, u32[]{:S(2)}, u32[]{:S(2)}) collective-permute-start(f32[768,256]{1,0:T(8,128)S(1)} %get-tuple-element.25), channel_id=1, source_target_pairs={{0,1},{1,0},{2,3},{3,2},{4,8},{5,9},{6,10},{7,11},{8,4},{9,5},{10,... | collective-permute-start | bytes 2359304 | tf_op jit(solution)/shard_map/ppermute | solution.py:308
  15.7 26.6 %collective-permute-start.6 = (f32[128,256]{1,0:T(8,128)S(1)}, f32[128,256]{1,0:T(8,128)S(1)}, u32[]{:S(2)}, u32[]{:S(2)}) collective-permute-start(f32[128,256]{1,0:T(8,128)S(1)} %get-tuple-element.32), channel_id=1, source_target_pairs={{0,4},{1,5},{2,6},{3,7},{4,0},{5,1},{6,2},{7,3},{8,12},{9,13},{10,... | collective-permute-start | bytes 393224 | tf_op jit(solution)/shard_map/ppermute | solution.py:308
  19.0 8.2 %collective-permute-start.1 = (f32[4,32,512]{2,1,0:T(8,128)S(1)}, f32[4,32,512]{2,1,0:T(8,128)S(1)}, u32[]{:S(2)}, u32[]{:S(2)}) collective-permute-start(f32[4,32,512]{2,1,0:T(8,128)S(1)} %add.3.p_ref), channel_id=1, source_target_pairs={{0,2},{1,3},{2,0},{3,1},{4,6},{5,7},{6,4},{7,5},{8,10},{9,11},{10,... | collective-permute-start | bytes 786440 | tf_op jit(solution)/shard_map/ppermute | solution.py:296
  20.5 7.0 %copy-start.7 = (f32[8,16,16]{2,1,0:T(8,128)S(1)}, f32[8,16,16]{2,1,0:T(8,128)}, u32[]{:S(2)}) copy-start(f32[8,16,16]{2,1,0:T(8,128)} %core_ref.3) | copy-start | bytes 24580
  27.1 13.5 %collective-permute-start.4 = (f32[192,256]{1,0:T(8,128)S(1)}, f32[192,256]{1,0:T(8,128)S(1)}, u32[]{:S(2)}, u32[]{:S(2)}) collective-permute-start(f32[192,256]{1,0:T(8,128)S(1)} %shard_map.124), channel_id=1, source_target_pairs={{0,4},{1,5},{2,6},{3,7},{4,0},{5,1},{6,2},{7,3},{8,12},{9,13},{10,... | collective-permute-start | bytes 589832 | tf_op jit(solution)/shard_map/ppermute | solution.py:308
  27.5 13.2 %collective-permute-start.5 = (f32[192,256]{1,0:T(8,128)S(1)}, f32[192,256]{1,0:T(8,128)S(1)}, u32[]{:S(2)}, u32[]{:S(2)}) collective-permute-start(f32[192,256]{1,0:T(8,128)S(1)} %shard_map.124), channel_id=1, source_target_pairs={{0,1},{1,0},{2,3},{3,2},{4,8},{5,9},{6,10},{7,11},{8,4},{9,5},{10,... | collective-permute-start | bytes 589832 | tf_op jit(solution)/shard_map/ppermute | solution.py:308
  27.5 6.3 %copy-start.6 = (bf16[256,512]{1,0:T(8,128)(2,1)S(1)}, bf16[256,512]{1,0:T(8,128)(2,1)}, u32[]{:S(2)}) copy-start(bf16[256,512]{1,0:T(8,128)(2,1)} %constant.9.clone.fl_ref) | copy-start | bytes 786436
  33.6 8.7 %collective-permute-start.7 = (f32[128,256]{1,0:T(8,128)S(1)}, f32[128,256]{1,0:T(8,128)S(1)}, u32[]{:S(2)}, u32[]{:S(2)}) collective-permute-start(f32[128,256]{1,0:T(8,128)S(1)} %get-tuple-element.32), channel_id=1, source_target_pairs={{0,1},{1,0},{2,3},{3,2},{4,8},{5,9},{6,10},{7,11},{8,4},{9,5},{10,... | collective-permute-start | bytes 393224 | tf_op jit(solution)/shard_map/ppermute | solution.py:308

commit v3 on v2

--- a/solution.py
+++ b/solution.py
@@ -95,15 +95,18 @@
         copy.wait()
 
 
-def load_kernel(tod_ref, *refs):
-    *parts, sem = refs
+def tail_copies(tod_ref, start, parts, sem):
     first = tod_ref.shape[1] - TAIL
-    copies, done = [], 0
+    copies = []
     for i, part in enumerate(parts):
-        there = slice(done, done + part.shape[0])
+        there = slice(start, start + part.shape[0])
         copies.append(pltpu.make_async_copy(tod_ref.at[there, first:], part, sem.at[i]))
-        done = there.stop
-    waited(started(copies))
+        start = there.stop
+    return started(copies)
+
+
+def load_kernel(tod_ref, out_ref, sem):
+    waited(tail_copies(tod_ref, 0, [out_ref], sem))
 
 
 def project_kernel(
@@ -140,7 +143,12 @@
             p_ref[j, part_idx * KMAX : (part_idx + 1) * KMAX, :] = total
 
 
-def prepare_kernel(vt_ref, wt_ref, mask_ref, coef_ref, v_ref, w_ref, levels_ref):
+def prepare_kernel(
+    tod_ref, vt_ref, wt_ref, mask_ref, coef_ref, v_ref, w_ref, levels_ref, middle_ref, late_ref, sem
+):
+    parts = [middle_ref, late_ref]
+    start = tod_ref.shape[0] - sum(part.shape[0] for part in parts)
+    copies = tail_copies(tod_ref, start, parts, sem)
     mask = jnp.concatenate([mask_ref[...]] * 3, 0).astype(BF16)
     across = (((0,), (0,)), ((), ()))
     levels_ref[...] = lax.dot_general(
@@ -152,6 +160,12 @@
         w_ref[here, :] = lax.dot_general(
             three(wt_ref[:, here]), one_each, across, preferred_element_type=F32
         )
+    waited(copies)
+
+
+def back(spectra, ih, il):
+    even = dot3(split(spectra[:, :BINS]), (ih[:BINS], il[:BINS]))
+    return even + dot3(split(spectra[:, BINS:]), (ih[BINS:], il[BINS:]))
 
 
 def filtered(pairs, w, tables):
@@ -204,9 +218,13 @@
     sums = [p_ref[j] + q_ref[j] for j in range(segs)]
     mask, levels, core = mask_ref[...], levels_ref[...], core_ref[...]
     rows = [to_correct(mask, a, b, core, levels) for a, b in zip(sums, sums[1:])]
-    z = dot3(split(jnp.concatenate(rows, 0)), (ih_ref[...], il_ref[...]))
-    z = split(jnp.concatenate([z[g * COLS : (g + 1) * COLS] for g in range(segs - 1)], 1))
-    out_ref[...] = main_ref[...] - dot3((v_ref[:, :COLS], v_ref[:, COLS:]), z)
+    z = split(back(jnp.concatenate(rows, 0), ih_ref[...], il_ref[...]))
+    for g in range(segs - 1):
+        own = z[0][g * COLS : (g + 1) * COLS], z[1][g * COLS : (g + 1) * COLS]
+        cols = slice(g * STEP, (g + 1) * STEP)
+        for here in rows_of(out_ref, 512):
+            off = dot3((v_ref[here, :COLS], v_ref[here, COLS:]), own)
+            out_ref[here, cols] = main_ref[here, cols] - off
 
 
 def came(odd, even):
@@ -243,13 +261,15 @@
     rows = to_correct(
         mask_ref[...], before, p_ref[0] + q_ref[0], core_ref[...], levels_ref[...]
     )
-    z = split(dot3(split(rows), tables[2:]))
+    z = split(back(rows, *tables[2:]))
     pair = sent[: done - soon], tod_ref[soon:done, :STEP]
     own = filtered([pair], w_ref[soon:done, :], tables)
-    off = dot3((v_ref[:, :COLS], v_ref[:, COLS:]), z)
-    out_ref[:soon, :] = soon_ref[...] - off[:soon]
-    out_ref[soon:, :] = own - off[soon:done]
-    off_ref[...] = off[done:]
+    half = soon // 2
+    for here in (slice(0, half), slice(half, soon)):
+        out_ref[here, :] = soon_ref[here, :] - dot3((v_ref[here, :COLS], v_ref[here, COLS:]), z)
+    off = dot3((v_ref[soon:, :COLS], v_ref[soon:, COLS:]), z)
+    out_ref[soon:, :] = own - off[: done - soon]
+    off_ref[...] = off[done - soon :]
     copy.wait()
 
 
@@ -313,7 +333,7 @@
     segs = samples // STEP
     known = samples - TAIL
     fh, fl, ih, il = tables = make_tables()
-    late = middle = dets // 8
+    late, middle = dets // 8, dets // 16
     soon = dets - late - middle
     whole = jax.ShapeDtypeStruct((dets, samples), F32)
 
@@ -324,17 +344,17 @@
         mode_counts.reshape(1, BANDS),
         band_edges.reshape(1, BANDS + 1),
     )
-    tails = run(
+    tail = run(
         load_kernel,
         (tod,),
         (),
-        tuple(pltpu.VMEM((count, TAIL), F32) for count in (soon, middle, late)),
-        scratch=[pltpu.SemaphoreType.DMA((3,))],
+        pltpu.VMEM((soon, TAIL), F32),
+        scratch=[pltpu.SemaphoreType.DMA((1,))],
         flops=int(2e10),
-        nbytes=8 * dets * TAIL,
-    )
-    odd_soon = pair_swap(tails[0], 0)
-    even_soon = pair_swap(tails[0], 1)
+        nbytes=8 * soon * TAIL,
+    )
+    odd_soon = pair_swap(tail, 0)
+    even_soon = pair_swap(tail, 1)
 
     sums, vt, mask = run(
         project_kernel,
@@ -348,15 +368,18 @@
         flops=6 * dets * COLS * samples,
         nbytes=4 * dets * samples,
     )
-    v, w, levels = run(
+    v, w, levels, middle_tail, late_tail = run(
         prepare_kernel,
-        (),
+        (tod,),
         (vt, small[0], mask, block_coef),
         (
             pltpu.VMEM((dets, 2 * COLS), BF16),
             pltpu.VMEM((dets, BINS), F32),
             pltpu.VMEM((NBLK, 2 * BINS), F32),
+            pltpu.VMEM((middle, TAIL), F32),
+            pltpu.VMEM((late, TAIL), F32),
         ),
+        scratch=[pltpu.SemaphoreType.DMA((2,))],
         flops=6 * dets * COLS * BANDS,
         nbytes=8 * dets * COLS,
     )
@@ -378,14 +401,14 @@
     packed = run(
         pack_kernel,
         (),
-        (tails[1], own, other),
+        (middle_tail, own, other),
         pltpu.VMEM((middle + 2 * ROWS, TAIL), F32),
         nbytes=8 * middle * TAIL,
     )
     odd_middle = pair_swap(packed, 0)
     even_middle = pair_swap(packed, 1)
-    odd_late = pair_swap(tails[2], 0)
-    even_late = pair_swap(tails[2], 1)
+    odd_late = pair_swap(late_tail, 0)
+    even_late = pair_swap(late_tail, 1)
 
     rest = run(
         rest_kernel,

time: 43.9 us -> 32.1 us (0.73)
  local copies, waits for them, and re-layouts: 7.91 us -> 0.06 us
  waiting for transfers between devices: 7.85 us -> 3.72 us
    unnamed x28 -> x26, local copies, waits for them, and re-layouts: 7.91 us -> 0.06 us
    ppermute x6, waiting for transfers between devices: 7.33 us -> 3.01 us  [pair_swap(): return lax.ppermute(block, ('tm', 'wafer'), route)]
  transfers between devices with their start and end apart: 8 -> 8, of which waited for: 3 -> 3; matrix products, arithmetic and copies ran while one was open for 0% -> 0% of each run, Pallas kernels for 35% -> 54%
where the time goes in v3:
time: 32.1 us; the launch traced here: 32 us
  Pallas kernels  19.7 us (61%)
  starting transfers between devices  8.26 us (26%)
  waiting for transfers between devices  3.72 us (12%)
    pallas_call x9, Pallas kernels, run(): pl.pallas_call(kernel, out_shape=outs, in_specs=[ANYWHERE] * len(loose) +...  19.7 us
    ppermute x6, starting transfers between devices, pair_swap(): return lax.ppermute(block, ('tm', 'wafer'), route)  6.15 us
    ppermute x6, waiting for transfers between devices, pair_swap(): return lax.ppermute(block, ('tm', 'wafer'), route)  3.01 us
    ppermute x2, starting transfers between devices, exchanged(): return lax.ppermute(block, axis, [(i, i ^ distance) for i in devices])  2.11 us
    ppermute x2, waiting for transfers between devices, exchanged(): return lax.ppermute(block, axis, [(i, i ^ distance) for i in devices])  0.71 us
  transfers between devices with their start and end apart: 8, of which 3 were waited for; matrix products, arithmetic and copies ran while one was open for 0% of the time, Pallas kernels for 54%

profile of v3, /device:TPU:0, one launch (start us, length us, event | category | flops | bytes accessed | tf_op | source)
XLA Modules:
  0.0 32.0 jit_solution(9598703294339734788)
XLA Ops:
  0.0 0.0 copy-start.4
  0.0 0.0 copy-start.5
  0.0 0.0 copy-start
  0.0 0.0 copy-start.7
  0.0 0.0 copy-start.10
  0.0 0.0 copy-start.11
  0.0 0.0 copy-start.12
  0.0 0.0 copy-start.9
  0.0 1.3 %shard_map.122 = f32[832,256]{1,0:T(8,128)S(1)} custom-call(f32[1024,1024]{1,0:T(8,128)} %tod_ref.13), custom_call_target="tpu_custom_call" | custom-call | flops 20000000000 | bytes 1703936 | tf_op jit(solution)/shard_map/pallas_call | solution.py:302
  1.4 0.0 copy-start.8
  1.4 3.1 %collective-permute-start.2 = (f32[832,256]{1,0:T(8,128)S(1)}, f32[832,256]{1,0:T(8,128)S(1)}, u32[]{:S(2)}, u32[]{:S(2)}) collective-permute-start(f32[832,256]{1,0:T(8,128)S(1)} %shard_map.122), channel_id=1, source_target_pairs={{0,4},{1,5},{2,6},{3,7},{4,0},{5,1},{6,2},{7,3},{8,12},{9,13},{10,... | collective-permute-start | bytes 2555912 | tf_op jit(solution)/shard_map/ppermute | solution.py:328
  4.5 0.0 collective-permute-start.3
  4.5 0.0 copy-done.4
  4.5 0.0 copy-done.5
  4.5 0.0 copy-done
  4.5 0.0 copy-done.7
  4.5 0.0 copy-done.10
  4.6 0.0 copy-done.11
  4.6 0.0 copy-done.12
  4.6 0.0 copy-done.9
  4.6 2.8 %shard_map.118 = (f32[4,32,512]{2,1,0:T(8,128)S(1)}, f32[256,1024]{1,0:T(8,128)S(1)}, f32[8,512]{1,0:T(8,128)S(1)}) custom-call(f32[1024,1024]{1,0:T(8,128)S(1)} %copy-done, f32[8,1024]{1,0:T(8,128)S(1)} %bitcast.4, f32[1024,128]{1,0:T(8,128)S(1)} %copy-done.9, s32[1,1024]{1,0:T(1,128)S(1)} %bitcast.6, s32[1,8]{1,0:T(1,128)S(1)} %bitcast.7, ...), custom_call_target="tpu_custom_call" | custom-call | flops 1610612736 | bytes 4194304 | tf_op jit(solution)/shard_map/pallas_call | solution.py:302
  7.4 0.0 copy-start.1
  7.4 0.0 copy-start.2
  7.4 0.0 copy-start.3
  7.4 0.6 %collective-permute-start = (f32[4,32,512]{2,1,0:T(8,128)S(1)}, f32[4,32,512]{2,1,0:T(8,128)S(1)}, u32[]{:S(2)}, u32[]{:S(2)}) collective-permute-start(f32[4,32,512]{2,1,0:T(8,128)S(1)} %get-tuple-element.21), channel_id=1, source_target_pairs={{0,1},{1,0},{2,3},{3,2},{4,5},{5,4},{6,7},{7,6},{8,9},{9,8},{10,11... | collective-permute-start | bytes 786440 | tf_op jit(solution)/shard_map/ppermute | solution.py:316
  8.0 0.0 copy-done.8
  8.0 1.5 %shard_map.119 = (bf16[1024,512]{1,0:T(8,128)(2,1)S(1)}, f32[1024,256]{1,0:T(8,128)S(1)}, f32[16,512]{1,0:T(8,128)S(1)}, f32[64,256]{1,0:T(8,128)S(1)}, f32[128,256]{1,0:T(8,128)S(1)}) custom-call(f32[1024,1024]{1,0:T(8,128)} %tod_ref.13, f32[256,1024]{1,0:T(8,128)S(1)} %get-tuple-element.18.vt_ref, f32[8,1024]{1,0:T(8,128)S(1)} %bitcast.5, ...), custom_call_target="tpu_custom_call" | custom-call | flops 12582912 | bytes 2097152 | tf_op jit(solution)/shard_map/pallas_call | solution.py:302
  9.5 2.5 %collective-permute-start.6 = (f32[128,256]{1,0:T(8,128)S(1)}, f32[128,256]{1,0:T(8,128)S(1)}, u32[]{:S(2)}, u32[]{:S(2)}) collective-permute-start(f32[128,256]{1,0:T(8,128)S(1)} %get-tuple-element.30), channel_id=1, source_target_pairs={{0,4},{1,5},{2,6},{3,7},{4,0},{5,1},{6,2},{7,3},{8,12},{9,13},{10,... | collective-permute-start | bytes 393224 | tf_op jit(solution)/shard_map/ppermute | solution.py:328
  12.0 0.0 collective-permute-done
  12.0 1.6 %collective-permute-start.1 = (f32[4,32,512]{2,1,0:T(8,128)S(1)}, f32[4,32,512]{2,1,0:T(8,128)S(1)}, u32[]{:S(2)}, u32[]{:S(2)}) collective-permute-start(f32[4,32,512]{2,1,0:T(8,128)S(1)} %add.3.p_ref), channel_id=1, source_target_pairs={{0,2},{1,3},{2,0},{3,1},{4,6},{5,7},{6,4},{7,5},{8,10},{9,11},{10,... | collective-permute-start | bytes 786440 | tf_op jit(solution)/shard_map/ppermute | solution.py:316
  13.6 0.0 copy-done.1
  13.6 0.0 copy-done.2
  13.6 0.0 copy-done.3
  13.6 0.0 copy-start.6
  13.6 6.1 %shard_map.120.main_ref = f32[1024,768]{1,0:T(8,128)S(1)} custom-call(f32[1024,1024]{1,0:T(8,128)S(1)} %copy-done.1, f32[1024,256]{1,0:T(8,128)S(1)} %get-tuple-element.20.w_ref, bf16[256,512]{1,0:T(8,128)(2,1)S(1)} %copy-done.4, bf16[256,512]{1,0:T(8,128)(2,1)S(1)} %copy-done.5, bf16[512,256]{1,0:T(8,128)(2,1)S(1)} %copy-done.2, bf16[512,256]{1,0:T(8,128)(2,1)S(1)} %copy-done.3), custom_call_target="tpu_custom_call" | custom-call | flops 4831838208 | bytes 7340032 | tf_op jit(solution)/shard_map/pallas_call | solution.py:302
  19.7 0.7 %collective-permute-done.1.q_ref = f32[4,32,512]{2,1,0:T(8,128)S(1)} collective-permute-done((f32[4,32,512]{2,1,0:T(8,128)S(1)}, f32[4,32,512]{2,1,0:T(8,128)S(1)}, u32[]{:S(2)}, u32[]{:S(2)}) %collective-permute-start.1) | collective-permute-done | bytes 262176 | tf_op jit(solution)/shard_map/ppermute | solution.py:316
  20.4 0.4 %collective-permute-start.4 = (f32[128,256]{1,0:T(8,128)S(1)}, f32[128,256]{1,0:T(8,128)S(1)}, u32[]{:S(2)}, u32[]{:S(2)}) collective-permute-start(f32[128,256]{1,0:T(8,128)S(1)} %shard_map.124), channel_id=1, source_target_pairs={{0,4},{1,5},{2,6},{3,7},{4,0},{5,1},{6,2},{7,3},{8,12},{9,13},{10,... | collective-permute-start | bytes 393224 | tf_op jit(solution)/shard_map/ppermute | solution.py:328
  20.8 0.0 collective-permute-start.5
  20.8 0.0 copy-done.6
  20.8 3.1 %shard_map.121.rest_ref = f32[1024,768]{1,0:T(8,128)S(1)} custom-call(f32[1024,768]{1,0:T(8,128)S(1)} %shard_map.120.main_ref, f32[4,32,512]{2,1,0:T(8,128)S(1)} %add.3.p_ref, f32[4,32,512]{2,1,0:T(8,128)S(1)} %collective-permute-done.1.q_ref, bf16[1024,512]{1,0:T(8,128)(2,1)S(1)} %get-tuple-element.22.v_ref, f32[8,512]{1,0:T(8,128)S(1)} %get-tuple-element.19.mask_ref, ...), custom_call_target="tpu_custom_call" | custom-call | flops 1207959552 | bytes 4194304 | tf_op jit(solution)/shard_map/pallas_call | solution.py:302
  23.9 0.4 %collective-permute-done.2.odd_ref = f32[832,256]{1,0:T(8,128)S(1)} collective-permute-done((f32[832,256]{1,0:T(8,128)S(1)}, f32[832,256]{1,0:T(8,128)S(1)}, u32[]{:S(2)}, u32[]{:S(2)}) %collective-permute-start.2) | collective-permute-done | bytes 852000 | tf_op jit(solution)/shard_map/ppermute | solution.py:328
  24.3 0.1 collective-permute-start.7
  24.4 0.0 collective-permute-done.3.even_ref
  24.4 2.1 %shard_map.123 = (f32[1024,1024]{1,0:T(8,128)}, f32[832,256]{1,0:T(8,128)S(1)}) custom-call(f32[1024,768]{1,0:T(8,128)S(1)} %shard_map.121.rest_ref, f32[832,256]{1,0:T(8,128)S(1)} %collective-permute-done.2.odd_ref, f32[832,256]{1,0:T(8,128)S(1)} %collective-permute-done.3.even_ref, f32[1024,1024]{1,0:T(8,128)S(1)} %copy-done.1, ...), custom_call_target="tpu_custom_call" | custom-call | flops 1308622848 | bytes 1703936 | tf_op jit(solution)/shard_map/pallas_call | solution.py:302
  26.5 2.5 %collective-permute-done.4.odd_ref = f32[128,256]{1,0:T(8,128)S(1)} collective-permute-done((f32[128,256]{1,0:T(8,128)S(1)}, f32[128,256]{1,0:T(8,128)S(1)}, u32[]{:S(2)}, u32[]{:S(2)}) %collective-permute-start.4) | collective-permute-done | bytes 131104 | tf_op jit(solution)/shard_map/ppermute | solution.py:328
  29.1 0.0 collective-permute-done.5.even_ref
  29.1 1.6 %shard_map.125 = (f32[1024,1024]{1,0:T(8,128)}, f32[896,256]{1,0:T(8,128)S(1)}, f32[128,256]{1,0:T(8,128)S(1)}) custom-call(f32[1024,1024]{1,0:T(8,128)} %get-tuple-element.24._, f32[1024,768]{1,0:T(8,128)S(1)} %shard_map.121.rest_ref, f32[832,256]{1,0:T(8,128)S(1)} %get-tuple-element.25.soon_ref, ...), custom_call_target="tpu_custom_call", output_to_operand_aliasing={{0}: (0, {})} | custom-call | flops 536870912 | bytes 1048576 | tf_op jit(solution)/shard_map/pallas_call | solution.py:302
  30.7 0.0 collective-permute-done.6.odd_ref
  30.7 0.0 collective-permute-done.7.even_ref
  30.7 1.2 %shard_map.126 = f32[1024,1024]{1,0:T(8,128)} custom-call(f32[1024,1024]{1,0:T(8,128)} %get-tuple-element.27._, f32[896,256]{1,0:T(8,128)S(1)} %get-tuple-element.28.most_ref, f32[128,256]{1,0:T(8,128)S(1)} %get-tuple-element.29.off_ref, f32[128,256]{1,0:T(8,128)S(1)} %collective-permute-done.6.odd_ref, ...), custom_call_target="tpu_custom_call", output_to_operand_aliasing={{}: (0, {})} | custom-call | flops 201326592 | bytes 2097152 | tf_op jit(solution)/shard_map/pallas_call | solution.py:302
  (2 shorter events, 0.1 us)
Async XLA Ops:
  0.0 4.5 %copy-start.4 = (bf16[256,512]{1,0:T(8,128)(2,1)S(1)}, bf16[256,512]{1,0:T(8,128)(2,1)}, u32[]{:S(2)}) copy-start(bf16[256,512]{1,0:T(8,128)(2,1)} %constant.8.clone.fh_ref) | copy-start | bytes 786436
  0.0 4.5 %copy-start.5 = (bf16[256,512]{1,0:T(8,128)(2,1)S(1)}, bf16[256,512]{1,0:T(8,128)(2,1)}, u32[]{:S(2)}) copy-start(bf16[256,512]{1,0:T(8,128)(2,1)} %constant.9.clone.fl_ref) | copy-start | bytes 786436
  0.0 4.5 %copy-start = (f32[1024,1024]{1,0:T(8,128)S(1)}, f32[1024,1024]{1,0:T(8,128)}, u32[]{:S(2)}) copy-start(f32[1024,1024]{1,0:T(8,128)} %tod_ref.13) | copy-start | bytes 12582916
  0.0 4.5 %copy-start.7 = (f32[1024,8]{0,1:T(8,128)S(1)}, f32[1024,8]{0,1:T(8,128)}, u32[]{:S(2)}) copy-start(f32[1024,8]{0,1:T(8,128)} %param.13) | copy-start | bytes 98308
  0.0 4.5 %copy-start.10 = (s32[1024]{0:T(1024)S(1)}, s32[1024]{0:T(1024)}, u32[]{:S(2)}) copy-start(s32[1024]{0:T(1024)} %param.18) | copy-start | bytes 12292
  0.0 4.5 %copy-start.11 = (s32[8]{0:T(128)S(1)}, s32[8]{0:T(128)}, u32[]{:S(2)}) copy-start(s32[8]{0:T(128)} %param.15) | copy-start | bytes 100
  0.0 4.5 %copy-start.12 = (s32[9]{0:T(128)S(1)}, s32[9]{0:T(128)}, u32[]{:S(2)}) copy-start(s32[9]{0:T(128)} %param.19) | copy-start | bytes 112
  0.0 4.5 %copy-start.9 = (f32[1024,128]{1,0:T(8,128)S(1)}, f32[1024,128]{1,0:T(8,128)}, u32[]{:S(2)}) copy-start(f32[1024,128]{1,0:T(8,128)} %modes_ref.1) | copy-start | bytes 1572868
  1.4 6.6 %copy-start.8 = (f32[8,16]{1,0:T(8,128)S(1)}, f32[8,16]{1,0:T(8,128)}, u32[]{:S(2)}) copy-start(f32[8,16]{1,0:T(8,128)} %coef_ref.1) | copy-start | bytes 1540
  1.4 22.9 %collective-permute-start.2 = (f32[832,256]{1,0:T(8,128)S(1)}, f32[832,256]{1,0:T(8,128)S(1)}, u32[]{:S(2)}, u32[]{:S(2)}) collective-permute-start(f32[832,256]{1,0:T(8,128)S(1)} %shard_map.122), channel_id=1, source_target_pairs={{0,4},{1,5},{2,6},{3,7},{4,0},{5,1},{6,2},{7,3},{8,12},{9,13},{10,... | collective-permute-start | bytes 2555912 | tf_op jit(solution)/shard_map/ppermute | solution.py:328
  4.5 19.9 %collective-permute-start.3 = (f32[832,256]{1,0:T(8,128)S(1)}, f32[832,256]{1,0:T(8,128)S(1)}, u32[]{:S(2)}, u32[]{:S(2)}) collective-permute-start(f32[832,256]{1,0:T(8,128)S(1)} %shard_map.122), channel_id=1, source_target_pairs={{0,1},{1,0},{2,3},{3,2},{4,8},{5,9},{6,10},{7,11},{8,4},{9,5},{10,... | collective-permute-start | bytes 2555912 | tf_op jit(solution)/shard_map/ppermute | solution.py:328
  7.4 6.2 %copy-start.1 = (f32[1024,1024]{1,0:T(8,128)S(1)}, f32[1024,1024]{1,0:T(8,128)}, u32[]{:S(2)}) copy-start(f32[1024,1024]{1,0:T(8,128)} %tod_ref.13) | copy-start | bytes 12582916
  7.4 6.2 %copy-start.2 = (bf16[512,256]{1,0:T(8,128)(2,1)S(1)}, bf16[512,256]{1,0:T(8,128)(2,1)}, u32[]{:S(2)}) copy-start(bf16[512,256]{1,0:T(8,128)(2,1)} %constant.10.clone.ih_ref) | copy-start | bytes 786436
  7.4 6.2 %copy-start.3 = (bf16[512,256]{1,0:T(8,128)(2,1)S(1)}, bf16[512,256]{1,0:T(8,128)(2,1)}, u32[]{:S(2)}) copy-start(bf16[512,256]{1,0:T(8,128)(2,1)} %constant.11.clone.il_ref) | copy-start | bytes 786436
  7.4 4.6 %collective-permute-start = (f32[4,32,512]{2,1,0:T(8,128)S(1)}, f32[4,32,512]{2,1,0:T(8,128)S(1)}, u32[]{:S(2)}, u32[]{:S(2)}) collective-permute-start(f32[4,32,512]{2,1,0:T(8,128)S(1)} %get-tuple-element.21), channel_id=1, source_target_pairs={{0,1},{1,0},{2,3},{3,2},{4,5},{5,4},{6,7},{7,6},{8,9},{9,8},{10,11... | collective-permute-start | bytes 786440 | tf_op jit(solution)/shard_map/ppermute | solution.py:316
  9.5 21.3 %collective-permute-start.6 = (f32[128,256]{1,0:T(8,128)S(1)}, f32[128,256]{1,0:T(8,128)S(1)}, u32[]{:S(2)}, u32[]{:S(2)}) collective-permute-start(f32[128,256]{1,0:T(8,128)S(1)} %get-tuple-element.30), channel_id=1, source_target_pairs={{0,4},{1,5},{2,6},{3,7},{4,0},{5,1},{6,2},{7,3},{8,12},{9,13},{10,... | collective-permute-start | bytes 393224 | tf_op jit(solution)/shard_map/ppermute | solution.py:328
  12.0 8.3 %collective-permute-start.1 = (f32[4,32,512]{2,1,0:T(8,128)S(1)}, f32[4,32,512]{2,1,0:T(8,128)S(1)}, u32[]{:S(2)}, u32[]{:S(2)}) collective-permute-start(f32[4,32,512]{2,1,0:T(8,128)S(1)} %add.3.p_ref), channel_id=1, source_target_pairs={{0,2},{1,3},{2,0},{3,1},{4,6},{5,7},{6,4},{7,5},{8,10},{9,11},{10,... | collective-permute-start | bytes 786440 | tf_op jit(solution)/shard_map/ppermute | solution.py:316
  13.6 7.2 %copy-start.6 = (f32[8,16,16]{2,1,0:T(8,128)S(1)}, f32[8,16,16]{2,1,0:T(8,128)}, u32[]{:S(2)}) copy-start(f32[8,16,16]{2,1,0:T(8,128)} %core_ref.3) | copy-start | bytes 24580
  20.4 8.7 %collective-permute-start.4 = (f32[128,256]{1,0:T(8,128)S(1)}, f32[128,256]{1,0:T(8,128)S(1)}, u32[]{:S(2)}, u32[]{:S(2)}) collective-permute-start(f32[128,256]{1,0:T(8,128)S(1)} %shard_map.124), channel_id=1, source_target_pairs={{0,4},{1,5},{2,6},{3,7},{4,0},{5,1},{6,2},{7,3},{8,12},{9,13},{10,... | collective-permute-start | bytes 393224 | tf_op jit(solution)/shard_map/ppermute | solution.py:328
  20.8 8.3 %collective-permute-start.5 = (f32[128,256]{1,0:T(8,128)S(1)}, f32[128,256]{1,0:T(8,128)S(1)}, u32[]{:S(2)}, u32[]{:S(2)}) collective-permute-start(f32[128,256]{1,0:T(8,128)S(1)} %shard_map.124), channel_id=1, source_target_pairs={{0,1},{1,0},{2,3},{3,2},{4,8},{5,9},{6,10},{7,11},{8,4},{9,5},{10,... | collective-permute-start | bytes 393224 | tf_op jit(solution)/shard_map/ppermute | solution.py:328
  24.3 6.4 %collective-permute-start.7 = (f32[128,256]{1,0:T(8,128)S(1)}, f32[128,256]{1,0:T(8,128)S(1)}, u32[]{:S(2)}, u32[]{:S(2)}) collective-permute-start(f32[128,256]{1,0:T(8,128)S(1)} %get-tuple-element.30), channel_id=1, source_target_pairs={{0,1},{1,0},{2,3},{3,2},{4,8},{5,9},{6,10},{7,11},{8,4},{9,5},{10,... | collective-permute-start | bytes 393224 | tf_op jit(solution)/shard_map/ppermute | solution.py:328
